TPU v7x, 512 devices: a whole 4x8x8 slice. The times are simulated.
512 devices in a mesh: kv: 4 (over x), blk: 128 (over z, y, core).
Axes of the slice: x: 4, y: 8, z: 8, core: 2. Of those that a mesh axis runs over, the one named last changes fastest.
Arguments:
- prefix_pool: bfloat16 [4, 3072, 64, 512], P('kv', 'blk'), may hold values from -6 to 6
- slot_page: int32 [3072], P('blk'), may hold values from 0 to 3071, as said below
- prompt_len: int32 [48], replicated, may hold values from 1 to 32768, 193536 in all
- request_ids: int32 [768], replicated, may hold values from 0 to 767, each once
- tail_len: int32 [768], P('blk'), may hold values from 1 to 128, 49152 in all
- tail_cache: bfloat16 [4, 768, 128, 512], P('kv', 'blk'), may hold values from -6 to 6
- queries: bfloat16 [768, 2, 2048], P('blk', None, 'kv'), may hold values from -120 to 120
- new_kv: bfloat16 [4, 768, 2, 512], P('kv', 'blk'), may hold values from -5.1 to 5.1
- hidden: bfloat16 [768, 2, 2048], P('blk'), may hold values from -4 to 4
- out_weight: bfloat16 [2048, 2048], P('kv'), may hold values from -0.125 to 0.125
- norm_gain: float32 [2048], replicated, may hold values from 0.1 to 1.9
- score_weight: float32 [2048], replicated, may hold values from -0.125 to 0.125
Outputs:
- hidden_out: bfloat16 [768, 2, 2048], P('blk')
- scores_out: float32 [768], P('blk')
Inputs may be any that keep to these rules, and one draw needn't show every extreme that they name: `slot_page`: the pages of all prompts fit the pool; every logical page number appears once. Request slot r serves sample request_ids[r] % 16 of prompt request_ids[r] // 16; every pair once.
All inputs are finite; a program needn't handle non-finite values. No bound on the sum of `tail_len` on one device may be relied on, other than what follows from the above.
Results may differ from a plain program's by a relative error of at most 0.02.
Values may be sent and summed in bfloat16 or wider, within the bound.
A program may use at most 64 MiB of HBM per device.

v0:
```python
import jax
import jax.numpy as jnp
from jax import lax
from jax.sharding import PartitionSpec as P

SAMPLES = 16


NEG_FLOOR = -1e30


def page_layout(slot_page, prompt_len, page_tokens):
    needed = (prompt_len + page_tokens - 1) // page_tokens
    page_ends = jnp.cumsum(needed)
    page_starts = page_ends - needed
    page_owner = jnp.sum((slot_page[:, None] >= page_ends[None, :]).astype(jnp.int32), axis=1)
    in_use = page_owner < prompt_len.shape[0]
    page_owner = jnp.minimum(page_owner, prompt_len.shape[0] - 1)
    offset = slot_page - page_starts[page_owner]
    position = offset[:, None] * page_tokens + jnp.arange(page_tokens, dtype=jnp.int32)[None, :]
    live_keys = in_use[:, None] & (position < prompt_len[page_owner][:, None])
    return (page_owner, live_keys)


def home_slots(request_ids):
    total_count = request_ids.shape[0]
    return (
        jnp.zeros((total_count,), jnp.int32)
        .at[request_ids]
        .set(jnp.arange(total_count, dtype=jnp.int32))
    )


def own_attention(
    own_queries, tail_block, fresh_block, tail_len, prefix_peak, prefix_num, prefix_den
):
    req_count, drafts, head_width = own_queries.shape
    head_size = tail_block.shape[2] // 2
    group_size = head_width // head_size
    row_count = drafts * group_size
    score_scale = head_size ** (-0.5)
    flat_queries = own_queries.reshape(req_count, row_count, head_size)
    tail_logits = (
        jnp.einsum(
            "rqh,rkh->rqk",
            flat_queries,
            tail_block[:, :, :head_size],
            preferred_element_type=jnp.float32,
        )
        * score_scale
    )
    tail_live = (jnp.arange(tail_block.shape[1], dtype=jnp.int32)[None, :] < tail_len[:, None])[
        :, None, :
    ]
    tail_logits = jnp.where(tail_live, tail_logits, NEG_FLOOR)
    fresh_logits = (
        jnp.einsum(
            "rqh,rkh->rqk",
            flat_queries,
            fresh_block[:, :, :head_size],
            preferred_element_type=jnp.float32,
        )
        * score_scale
    )
    fresh_live = (
        jnp.arange(drafts, dtype=jnp.int32)[None, :]
        <= (jnp.arange(row_count, dtype=jnp.int32) // group_size)[:, None]
    )[None]
    fresh_logits = jnp.where(fresh_live, fresh_logits, NEG_FLOOR)
    own_peak = jnp.maximum(jnp.max(tail_logits, axis=2), jnp.max(fresh_logits, axis=2))
    top_peak = jnp.maximum(prefix_peak, own_peak)
    tail_weights = jnp.where(tail_live, jnp.exp(tail_logits - top_peak[:, :, None]), 0.0)
    fresh_weights = jnp.where(fresh_live, jnp.exp(fresh_logits - top_peak[:, :, None]), 0.0)
    carried = jnp.exp(prefix_peak - top_peak)
    numer = prefix_num * carried[:, :, None]
    numer = numer + jnp.einsum(
        "rqk,rkh->rqh",
        tail_weights.astype(jnp.bfloat16),
        tail_block[:, :, head_size:],
        preferred_element_type=jnp.float32,
    )
    numer = numer + jnp.einsum(
        "rqk,rkh->rqh",
        fresh_weights.astype(jnp.bfloat16),
        fresh_block[:, :, head_size:],
        preferred_element_type=jnp.float32,
    )
    denom = prefix_den * carried + jnp.sum(tail_weights, axis=2) + jnp.sum(fresh_weights, axis=2)
    return (numer / denom[:, :, None]).astype(jnp.bfloat16).reshape(req_count, drafts, head_width)


def page_sums(
    logits, live_keys, slot_rows, peak_table, page_pool, total_count, row_count, head_size
):
    page_count = page_pool.shape[0]
    flat_rows = slot_rows.reshape(-1)
    ref_peak = peak_table[slot_rows].reshape(page_count, -1)
    weights = jnp.where(live_keys[:, None, :], jnp.exp(logits - ref_peak[:, :, None]), 0.0)
    slot_den = jnp.sum(weights, axis=2).reshape(-1, row_count)
    slot_num = jnp.einsum(
        "prk,pkh->prh",
        weights.astype(jnp.bfloat16),
        page_pool[:, :, head_size:],
        preferred_element_type=jnp.float32,
    ).reshape(-1, row_count, head_size)
    prefix_num = (
        jnp.zeros((total_count, row_count, head_size), jnp.float32).at[flat_rows].add(slot_num)
    )
    prefix_den = jnp.zeros((total_count, row_count), jnp.float32).at[flat_rows].add(slot_den)
    return (prefix_num, prefix_den)


def body(
    prefix_pool,
    slot_page,
    prompt_len,
    request_ids,
    tail_len,
    tail_cache,
    queries,
    new_kv,
    hidden,
    out_weight,
    norm_gain,
    score_weight,
):
    page_pool = prefix_pool[0]
    page_count = page_pool.shape[0]
    page_tokens = page_pool.shape[1]
    head_size = page_pool.shape[2] // 2
    local_count, drafts, head_width = queries.shape
    group_size = head_width // head_size
    row_count = drafts * group_size
    total_count = request_ids.shape[0]
    score_scale = head_size ** (-0.5)
    page_owner, live_keys = page_layout(slot_page, prompt_len, page_tokens)
    home_rows = home_slots(request_ids)
    slot_rows = home_rows[
        page_owner[:, None] * SAMPLES + jnp.arange(SAMPLES, dtype=jnp.int32)[None, :]
    ]
    all_queries = lax.all_gather(queries, "blk", axis=0, tiled=True)
    picked = all_queries[slot_rows].reshape(page_count, -1, head_size)
    logits = (
        jnp.einsum(
            "prh,pkh->prk", picked, page_pool[:, :, :head_size], preferred_element_type=jnp.float32
        )
        * score_scale
    )
    logits = jnp.where(live_keys[:, None, :], logits, NEG_FLOOR)
    flat_rows = slot_rows.reshape(-1)
    slot_peak = jnp.max(logits, axis=2).reshape(-1, row_count)
    local_peak = (
        jnp.full((total_count, row_count), NEG_FLOOR, jnp.float32).at[flat_rows].max(slot_peak)
    )
    row_start = lax.axis_index("blk") * local_count
    global_peak = lax.pmax(local_peak, "blk")
    prefix_num, prefix_den = page_sums(
        logits, live_keys, slot_rows, global_peak, page_pool, total_count, row_count, head_size
    )
    total_num, total_den = lax.psum((prefix_num, prefix_den), "blk")
    own_num = lax.dynamic_slice_in_dim(total_num, row_start, local_count, 0)
    own_den = lax.dynamic_slice_in_dim(total_den, row_start, local_count, 0)
    own_peak = lax.dynamic_slice_in_dim(global_peak, row_start, local_count, 0)
    attention = own_attention(
        queries, tail_cache[0], new_kv[0], tail_len, own_peak, own_num, own_den
    )
    partial_value = jnp.dot(
        attention.reshape(-1, head_width), out_weight, preferred_element_type=jnp.float32
    )
    summed = lax.psum(partial_value.astype(jnp.bfloat16), "kv").astype(jnp.float32)
    hidden_out = (hidden.astype(jnp.float32) + summed.reshape(hidden.shape)).astype(jnp.bfloat16)
    last_hidden = hidden_out[:, -1, :].astype(jnp.float32)
    normed = (
        last_hidden
        * lax.rsqrt(jnp.mean(last_hidden * last_hidden, axis=-1, keepdims=True) + 1e-06)
        * norm_gain
    )
    scores_out = jnp.sum(normed * score_weight, axis=-1)
    return (hidden_out, scores_out)


def solution(mesh):
    in_specs = (
        P("kv", "blk", None, None),
        P("blk"),
        P(),
        P(),
        P("blk"),
        P("kv", "blk", None, None),
        P("blk", None, "kv"),
        P("kv", "blk", None, None),
        P("blk", None, None),
        P("kv", None),
        P(),
        P(),
    )
    out_specs = (P("blk", None, None), P("blk"))
    return jax.shard_map(body, mesh=mesh, in_specs=in_specs, out_specs=out_specs, check_vma=False)
```

profile of v0, /device:TPU:1, one launch (start us, length us, event | category | flops | bytes accessed | tf_op | source)
XLA Modules:
  0.0 1170.7 jit_solution(3096349030965431922)
XLA Ops:
  7.2 0.7 all-gather.2.cloned.1.call-update
  8.0 0.7 fusion.50
  8.9 0.8 convert_reduce_fusion
  9.8 1.4 gather_fusion.2
  11.1 0.7 fusion.49
  11.8 0.7 gather_fusion.1
  12.7 0.7 compare_select_fusion.2
  13.4 3.4 scatter_custom_fusion
  16.8 1.9 gather_fusion
  19.0 80.7 %all-gather.2.cloned.1.call-done = bf16[768,2,512]{2,1,0:T(2,128)(2,1)} async-done(((bf16[6,2,512]{2,1,0:T(2,128)(2,1)}), bf16[768,2,512]{2,1,0:T(2,128)(2,1)}) %all-gather.2.cloned.1.call-update) | async-done | bytes 1572880 | tf_op jit(solution)/shard_map/all_gather | solution.py:141
  99.7 3.8 gather_fusion.3
  103.5 1.4 reshape.268
  104.9 1.8 fusion.41
  106.8 2.5 scatter_custom_fusion.1
  109.4 488.6 %pmax.7 = f32[768,4]{1,0:T(8,128)S(1)} all-reduce(f32[768,4]{1,0:T(8,128)} %scatter_custom_fusion.1), channel_id=1, replica_groups=mesh['kv'=4,'blk'=128] {'blk'}, use_global_device_ids=true, to_apply=%region_5.6 | all-reduce | flops 3072 | bytes 24576 | tf_op jit(solution)/shard_map/pmax | solution.py:156
  597.9 1.1 gather_fusion.4
  599.2 3.0 fusion.5
  602.2 2.7 reshape.336
  604.9 2.1 broadcast_in_dim.99
  607.0 43.5 %scatter_fusion = f32[768,4,256]{2,1,0:T(4,128)} fusion(f32[768,4,256]{2,1,0:T(4,128)} %broadcast_in_dim.99, s32[384]{0:T(512)S(1)} %fusion.36, f32[384,4,256]{2,1,0:T(4,128)} %reshape.336), kind=kCustom, calls=%fused_computation.7 | custom fusion | flops 393216 | bytes 4720128 | tf_op jit(solution)/shard_map/scatter-add | solution.py:107
  650.5 0.7 copy-done.1
  651.4 1.3 fusion.42
  652.6 0.3 fusion.8
  653.1 1.9 scatter_custom_fusion.3
  655.1 491.3 %psum.22 = f32[768,4]{1,0:T(8,128)S(1)} all-reduce(f32[768,4]{1,0:T(8,128)S(1)} %scatter_custom_fusion.3), channel_id=1, replica_groups=mesh['kv'=4,'blk'=128] {'blk'}, use_global_device_ids=true, to_apply=%region_12.13 | all-reduce | flops 3072 | bytes 24576 | tf_op jit(solution)/shard_map/psum | solution.py:160
  1146.4 0.2 fusion.25
  1146.6 1.2 convolution_add_fusion.1
  1147.9 0.2 fusion.2
  1148.1 0.4 convolution_convert_fusion
  1148.6 13.7 %psum.23 = bf16[6,2,2048]{2,0,1:T(8,128)(2,1)S(1)} all-reduce(bf16[6,2,2048]{2,0,1:T(8,128)(2,1)S(1)} %copy.29), channel_id=1, replica_groups=mesh['kv'=4,'blk'=128] {'kv'}, use_global_device_ids=true, to_apply=%region_15.16 | all-reduce | flops 24576 | bytes 98304 | tf_op jit(solution)/shard_map/psum | solution.py:170
  1162.5 0.7 copy.30
  1163.1 0.7 fusion.23
  (54 shorter events, 1.8 us)
Async XLA Ops:
  7.2 1140.9 %copy-start = (bf16[512,2048]{1,0:T(8,128)(2,1)S(1)}, bf16[512,2048]{1,0:T(8,128)(2,1)}, u32[]{:S(2)}) copy-start(bf16[512,2048]{1,0:T(8,128)(2,1)} %param.21) | copy-start | bytes 6291460
  7.2 92.6 %all-gather.2.cloned.1.call-start = ((), (), s32[]{:S(2)}) async-start(), calls=%async_computation | async-start | bytes 1585152 | tf_op jit(solution)/shard_map/all_gather | solution.py:141
  7.9 1138.7 %all-reduce.2.cloned.1.call-start = ((), (), s32[]{:S(2)}) async-start(), calls=%async_computation.1 | async-start | bytes 6291456 | tf_op jit(solution)/shard_map/psum | solution.py:160
  16.8 2.1 copy-start.6
  650.4 0.7 copy-start.1
  650.4 0.7 copy-start.7
  650.4 0.8 copy-start.5
  1146.6 15.7 %copy-start.2 = (bf16[6,2,2048]{2,1,0:T(2,128)(2,1)S(1)}, bf16[6,2,2048]{2,1,0:T(2,128)(2,1)}, u32[]{:S(2)}) copy-start(bf16[6,2,2048]{2,1,0:T(2,128)(2,1)} %param.20) | copy-start | bytes 147460
  1147.8 15.3 %copy-start.3 = (f32[2048]{0:T(1024)S(1)}, f32[2048]{0:T(1024)}, u32[]{:S(2)}) copy-start(f32[2048]{0:T(1024)} %param.23) | copy-start | bytes 24580
  1147.8 15.3 %copy-start.4 = (f32[2048]{0:T(1024)S(1)}, f32[2048]{0:T(1024)}, u32[]{:S(2)}) copy-start(f32[2048]{0:T(1024)} %param.22) | copy-start | bytes 24580
Sparse Core Ops, SparseCore 0:
  11.2 88.4 all-gather.1
  650.6 202.6 all-reduce.1
where the time goes:
time: 1180 us; the launch traced here: 1170 us
  blocking collectives  994 us (84%)
  waiting for transfers between devices  81.5 us (7%)
  other arithmetic  52.7 us (4%)
  local copies, waits for them, and re-layouts  20.6 us (2%)
  between operations  14.3 us (1%)
    psum x1, blocking collectives, body(): total_num, total_den = lax.psum((prefix_num, prefix_den), 'blk')  491 us
    pmax x1, blocking collectives, body(): global_peak = lax.pmax(local_peak, 'blk')  489 us
    all_gather x1, waiting for transfers between devices, body(): all_queries = lax.all_gather(queries, 'blk', axis=0, tiled=True)  80.7 us
    scatter-add x1, other arithmetic, page_sums(): jnp.zeros((total_count, row_count, head_size), jnp.float32).at[flat_rows]  43.5 us
  transfers between devices with their start and end apart: 2, of which 1 were waited for; matrix products, arithmetic and copies ran while one was open for 1% of the time, Pallas kernels for 0%

commit v1 on v0

v1 whole, which is shorter than its diff:
```python
import functools

import jax
import jax.numpy as jnp
from jax import lax
from jax.experimental import pallas as pl
from jax.experimental.pallas import tpu as pltpu
from jax.sharding import PartitionSpec as P

MESH = pl.DeviceIdType.MESH
SAMPLES = 16
HEAD = 256
PAGE = 64
NEG = -1e30
F32 = jnp.float32
BF16 = jnp.bfloat16


def iota(shape, dim):
    return lax.broadcasted_iota(jnp.int32, shape, dim)


def dot(a, b, ca=1, cb=0):
    return lax.dot_general(a, b, (((ca,), (cb,)), ((), ())), preferred_element_type=F32)


def split3(x):
    a = x.astype(BF16).astype(F32)
    b = (x - a).astype(BF16).astype(F32)
    return a, b, x - a - b


def kernel(
    n, nx, reqs, pages,
    slot_ref, plen_ref, tlen_ref, ids_ref, q_ref, nk_ref, hid_ref, gain_ref, score_ref,
    pool_hbm, tail_hbm, w_hbm,
    out_ref, sc_ref,
    poolv, tailv, wv, s1, agm, ago, gm, go, gtm, gto, pick, accb, stb,
    xo_acc, xo_st, rx_acc, rx_st, tx_acc, tx_ml, rs_acc, rs_ml, t2, r2,
    own_acc, own_st, part, ar,
    local_sem, s1_send, s1_recv, ag_send, ag_recv, fw_send, fw_recv,
    xo_send, xo_recv, xs_send, xs_recv, rs_send, rs_recv, rm_send, rm_recv,
    t2_send, t2_recv, ar_send, ar_recv,
):
    chunk = n * 2 * reqs
    rows = pages * SAMPLES
    prompts = plen_ref.shape[0]
    scale = HEAD ** (-0.5)
    x = lax.axis_index("kv")
    b = lax.axis_index("blk")
    k = lax.rem(b, 2)
    y = lax.rem(lax.div(b, 2), n)
    z = lax.div(b, 2 * n)
    p1 = y + k * (z - y)
    p2 = z + k * (y - z)
    other = 1 - k

    def at(zz, yy, kk):
        return (x, (zz * n + yy) * 2 + kk)

    def ring1(pos, h, kk):
        if h == 0:
            return at(z, pos, kk)
        return at(pos, y, kk)

    def mine1(pos, kk):
        return at(z + k * (pos - z), pos + k * (y - pos), kk)

    def mine2(pos):
        return at(pos + k * (z - pos), y + k * (pos - y), k)

    partner = at(z, y, other)

    def remote(src, dst, send, recv, to):
        return pltpu.make_async_remote_copy(
            src_ref=src, dst_ref=dst, send_sem=send, recv_sem=recv, device_id=to, device_id_type=MESH
        )

    barrier = pltpu.get_barrier_semaphore()

    def greet(to):
        pl.semaphore_signal(barrier, inc=1, device_id=to, device_id_type=MESH)

    greet(partner)
    for d in range(1, n):
        for kk in range(2):
            greet(at(z, lax.rem(y + d, n), kk))
            greet(at(lax.rem(z + d, n), y, kk))
    for d in range(1, nx):
        greet((lax.rem(x + d, nx), b))

    loads = [
        pltpu.make_async_copy(pool_hbm, poolv, local_sem.at[0]),
        pltpu.make_async_copy(tail_hbm, tailv, local_sem.at[1]),
        pltpu.make_async_copy(w_hbm, wv, local_sem.at[2]),
    ]
    for load in loads:
        load.start()
    s1[p1 * 2 + k] = q_ref[k]

    pl.semaphore_wait(barrier, 1 + 4 * (n - 1) + (nx - 1))

    def first(h, d):
        mypos = (y, z)[h]
        pos = lax.rem(mypos + d, n)
        slot = mypos * 2 + k
        return remote(
            q_ref.at[h], s1.at[slot], s1_send.at[h * n + d], s1_recv.at[slot], ring1(pos, h, h)
        )

    for d in range(1, n):
        for h in range(2):
            first(h, d).start()
    remote(q_ref.at[other], s1.at[remote_slot(n, y, z, k)], s1_send.at[other * n],
           s1_recv.at[remote_slot(n, y, z, k)], partner).start()

    lane = iota((1, 128), 1)
    lens = jnp.zeros((1, 128), jnp.int32)
    for p in range(prompts):
        lens = jnp.where(lane == p, plen_ref[p], lens)
    need = lax.div(lens + (PAGE - 1), PAGE).astype(F32)
    grid_r, grid_c = iota((128, 128), 0), iota((128, 128), 1)
    need_t = jnp.transpose(jnp.broadcast_to(need, (128, 128)))
    ends = jnp.sum(jnp.where(grid_r <= grid_c, need_t, 0.0), axis=0, keepdims=True)
    starts = ends - need
    page_r = iota((pages, 128), 0)
    slots = jnp.zeros((pages, 128), jnp.int32)
    for j in range(pages):
        slots = jnp.where(page_r == j, slot_ref[j], slots)
    slots = slots.astype(F32)
    plane = iota((pages, 128), 1)
    owner = jnp.sum(
        jnp.where((plane < prompts) & (slots >= ends), 1.0, 0.0), axis=1, keepdims=True
    )
    used = owner < prompts
    owner = jnp.minimum(owner, prompts - 1.0)
    mine = plane.astype(F32) == owner
    start = jnp.sum(jnp.where(mine, starts, 0.0), axis=1, keepdims=True)
    length = jnp.sum(jnp.where(mine, lens.astype(F32), 0.0), axis=1, keepdims=True)
    live = jnp.where(used, length - (slots - start) * PAGE, 0.0)

    sample = lax.rem(iota((rows, 128), 0), SAMPLES).astype(F32)
    target = (
        jnp.broadcast_to((owner * SAMPLES + jnp.zeros_like(slots))[:, None, :], (pages, SAMPLES, 128))
        .reshape(rows, 128) + sample
    )
    live_c = jnp.broadcast_to(live[:, None, :], (pages, SAMPLES, 128)).reshape(rows, 128)
    target_row = jnp.concatenate(
        [jnp.transpose(target[i * 128:(i + 1) * 128])[0:1] for i in range(rows // 128)], axis=1
    )
    live_row = jnp.concatenate(
        [jnp.transpose(live_c[i * 128:(i + 1) * 128])[0:1] for i in range(rows // 128)], axis=1
    )
    for half, g, gt in ((k, gm, gtm), (other, go, gto)):
        ids = ids_ref[half]
        padded = jnp.concatenate([ids, jnp.zeros((128 - n, 128), F32)], axis=0)
        ids_t = jnp.transpose(padded)
        for p in range(n):
            g[p] = jnp.where(
                target[:, :chunk] == ids[p:p + 1, :chunk], 1.0, 0.0
            ).astype(BF16)
            gt[pl.ds(p * chunk, chunk), :] = jnp.where(
                ids_t[:chunk, p:p + 1] == target_row, 1.0, 0.0
            ).astype(BF16)

    loads[1].wait()
    qown = jnp.concatenate([q_ref[0], q_ref[1]], axis=0)
    tails = tailv[...].reshape(reqs * 128, 2 * HEAD)
    news = nk_ref[...]
    row32 = lax.rem(iota((32, reqs * 128), 0), 8)
    col32 = iota((32, reqs * 128), 1)
    tl = jnp.concatenate([jnp.full((1, 128), tlen_ref[r], jnp.int32) for r in range(reqs)], axis=1)
    tlive = (row32 == lax.div(col32, 128)) & (lax.rem(col32, 128) < tl)
    ts = jnp.where(tlive, dot(qown, tails[:, :HEAD], 1, 1) * scale, NEG)
    nrow, ncol = iota((32, 16), 0), iota((32, 16), 1)
    nlive = (lax.rem(nrow, 8) == lax.rem(ncol, 8)) & (lax.div(ncol, 8) <= lax.div(nrow, 16))
    ns = jnp.where(nlive, dot(qown, news[:, :HEAD], 1, 1) * scale, NEG)
    peak = jnp.maximum(jnp.max(ts, axis=1, keepdims=True), jnp.max(ns, axis=1, keepdims=True))
    tw = jnp.where(tlive, jnp.exp(ts - peak), 0.0)
    nw = jnp.where(nlive, jnp.exp(ns - peak), 0.0)
    own_acc[...] = dot(tw.astype(BF16), tails[:, HEAD:]) + dot(nw.astype(BF16), news[:, HEAD:])
    own_den = jnp.sum(tw, axis=1, keepdims=True) + jnp.sum(nw, axis=1, keepdims=True)
    own_st[...] = jnp.where(iota((32, 128), 1) == 0, peak, own_den)

    for d in range(n):
        for kk in range(2):
            slot = lax.rem(p1 + d, n) * 2 + lax.rem(k + kk, 2)
            if d or kk:
                remote(q_ref.at[0], s1.at[slot], s1_send.at[0], s1_recv.at[slot], partner).wait_recv()
    s1v = s1[...].reshape(2 * n * 16, HEAD)
    pr, pc = iota((chunk, 2 * n * 16), 0), iota((chunk, 2 * n * 16), 1)
    want = lax.div(pr, reqs) * 16 + lax.rem(pr, reqs)
    packed = [
        dot(jnp.where(pc == want + c * 8, 1.0, 0.0).astype(BF16), s1v) for c in range(2)
    ]
    agm[p2] = jnp.concatenate(packed, axis=1).astype(BF16)

    def second(pos, src):
        return remote(agm.at[src], agm.at[src], ag_send.at[pos], ag_recv.at[src], mine2(pos))

    def forward(src):
        return remote(agm.at[src], ago.at[src], fw_send.at[src], fw_recv.at[src], partner)

    far = [d for i in range(1, n // 2 + 1) for d in ((i, n - i) if 2 * i != n else (i,))]
    for d in far:
        pos = lax.rem(p2 + d, n)
        second(pos, p2).start()
    forward(p2).start()
    pick[0] = dot(gm[p2], agm[p2])
    for d in far:
        src = lax.rem(p2 + n - d, n)
        second(src, src).wait_recv()
        forward(src).start()
        pick[0] += dot(gm[src], agm[src])
    q2 = p1
    for i, d in enumerate([0] + far):
        src = lax.rem(q2 + n - d, n)
        forward(src).wait_recv()
        got = dot(go[src], ago[src])
        pick[1] = got if i == 0 else pick[1] + got

    loads[0].wait()
    blocks = pages // 8
    scores, peaks = [], []
    for blk in range(blocks):
        keys = poolv[blk * 8:(blk + 1) * 8].reshape(8 * PAGE, 2 * HEAD)[:, :HEAD]
        qb = jnp.concatenate(
            [
                pick[h, blk * 128:(blk + 1) * 128, c * HEAD:(c + 1) * HEAD].astype(BF16)
                for h in range(2) for c in range(2)
            ],
            axis=0,
        )
        full = dot(keys, qb, 1, 1)
        page_l = lax.div(lax.rem(iota((PAGE, 512), 1), 128), SAMPLES)
        s = jnp.zeros((PAGE, 512), F32)
        for j in range(8):
            s = jnp.where(page_l == j, full[j * PAGE:(j + 1) * PAGE], s)
        lv = jnp.concatenate([live_row[:, blk * 128:(blk + 1) * 128]] * 4, axis=1)
        alive = iota((PAGE, 512), 0).astype(F32) < lv
        s = jnp.where(alive, s * scale, NEG)
        scores.append((s, alive))
        m = jnp.max(s, axis=0, keepdims=True)
        peaks.append(jnp.concatenate([m[:, i * 128:(i + 1) * 128] for i in range(4)], axis=0))
    local = jnp.concatenate(peaks, axis=1)
    local = jnp.concatenate([local, local], axis=0)
    tgt8 = jnp.broadcast_to(target_row, (8, rows))
    lane8 = iota((8, rows), 1)
    top = local
    lead = jnp.ones((8, rows), F32)
    for d in range(1, pages):
        same = pltpu.roll(tgt8, d * SAMPLES, 1) == tgt8
        top = jnp.where(same, jnp.maximum(top, pltpu.roll(local, d * SAMPLES, 1)), top)
        lead = jnp.where(same & (lane8 >= d * SAMPLES), 0.0, lead)
    dens = []
    for blk in range(blocks):
        s, alive = scores[blk]
        tb = top[:, blk * 128:(blk + 1) * 128]
        tb = jnp.concatenate([tb[i:i + 1] for i in range(4)], axis=1)
        w = jnp.where(alive, jnp.exp(s - tb), 0.0)
        dsum = jnp.sum(w, axis=0, keepdims=True)
        dens.append(jnp.concatenate([dsum[:, i * 128:(i + 1) * 128] for i in range(4)], axis=0))
        page_l = lax.div(lax.rem(iota((PAGE, 512), 1), 128), SAMPLES)
        wide = jnp.concatenate([jnp.where(page_l == j, w, 0.0) for j in range(8)], axis=0)
        values = poolv[blk * 8:(blk + 1) * 8].reshape(8 * PAGE, 2 * HEAD)[:, HEAD:]
        acc = dot(jnp.transpose(wide).astype(BF16), values)
        for h in range(2):
            for c in range(2):
                i = h * 2 + c
                accb[h, blk * 128:(blk + 1) * 128, c * HEAD:(c + 1) * HEAD] = (
                    acc[i * 128:(i + 1) * 128].astype(BF16)
                )
    den = jnp.concatenate(dens, axis=1)
    for h in range(2):
        ms = jnp.where(lead[0:2] > 0.5, top[2 * h:2 * h + 2], 0.0)
        st = jnp.concatenate(
            [ms, den[2 * h:2 * h + 2], lead[0:1], jnp.zeros((123, rows), F32)], axis=0
        )
        st = jnp.concatenate(
            [jnp.transpose(st[:, i * 128:(i + 1) * 128]) for i in range(rows // 128)], axis=0
        )
        stb[h] = jnp.concatenate([t.astype(BF16) for t in split3(st)], axis=1)

    lane_c = iota((chunk, 128), 1)

    def column_stats(g, h):
        st = dot(g, stb[h])
        st = st[:, :128] + st[:, 128:256] + st[:, 256:]
        return jnp.where((lane_c < 2) & (st[:, 4:5] < 0.5), NEG, st)

    for p in range(n):
        g = gto[pl.ds(p * chunk, chunk), :]
        xo_acc[p] = dot(g, accb[1]).astype(BF16)
        xo_st[p] = column_stats(g, 1)
        remote(xo_acc.at[p], rx_acc.at[p], xo_send.at[p], xo_recv.at[p], partner).start()
        remote(xo_st.at[p], rx_st.at[p], xs_send.at[p], xs_recv.at[p], partner).start()

    def spread(col):
        return jnp.broadcast_to(col, (chunk, HEAD))

    def to_ring_acc(p):
        return remote(tx_acc.at[p], rs_acc.at[p2], rs_send.at[p], rs_recv.at[p2], mine2(p))

    def to_ring_ml(p):
        return remote(tx_ml.at[p], rs_ml.at[p2], rm_send.at[p], rm_recv.at[p2], mine2(p))

    for d in far[::-1] + [0]:
        p = lax.rem(p2 + d, n)
        g = gtm[pl.ds(pl.multiple_of(p * chunk, chunk), chunk), :]
        acc = dot(g, accb[0])
        st = column_stats(g, 0)
        remote(xo_acc.at[p], rx_acc.at[p], xo_send.at[p], xo_recv.at[p], partner).wait_recv()
        remote(xo_st.at[p], rx_st.at[p], xs_send.at[p], xs_recv.at[p], partner).wait_recv()
        st2 = rx_st[p]
        both = jnp.maximum(st, st2)
        a, c2 = jnp.exp(st - both), jnp.exp(st2 - both)
        acc2 = rx_acc[p].astype(F32)
        outs, dn = [], []
        for c in range(2):
            sl = slice(c * HEAD, (c + 1) * HEAD)
            wa, wb = a[:, c:c + 1], c2[:, c:c + 1]
            outs.append(acc[:, sl] * spread(wa) + acc2[:, sl] * spread(wb))
            dn.append(st[:, 2 + c:3 + c] * wa + st2[:, 2 + c:3 + c] * wb)
        ml = jnp.where(lane_c < 2, both, jnp.where(lane_c == 2, dn[0], dn[1]))
        if chunk < 128:
            ml = jnp.concatenate([ml, jnp.zeros((128 - chunk, 128), F32)], axis=0)
        ml = jnp.transpose(ml)[0:8]
        outs = jnp.concatenate(outs, axis=1).astype(BF16)
        if d:
            tx_acc[p] = outs
            tx_ml[p] = ml
            to_ring_acc(p).start()
            to_ring_ml(p).start()
        else:
            rs_acc[p] = outs
            rs_ml[p] = ml

    for d in far:
        src = lax.rem(p2 + n - d, n)
        remote(tx_acc.at[src], rs_acc.at[src], rs_send.at[src], rs_recv.at[src], partner).wait_recv()
        remote(tx_ml.at[src], rs_ml.at[src], rm_send.at[src], rm_recv.at[src], partner).wait_recv()
    stats = []
    for c in range(2):
        m = jnp.concatenate([rs_ml[i, c:c + 1, :] for i in range(n)], axis=0)
        den_c = jnp.concatenate([rs_ml[i, 2 + c:3 + c, :] for i in range(n)], axis=0)
        mx = jnp.max(m, axis=0, keepdims=True)
        w = jnp.exp(m - mx)
        stats.append((w, mx, jnp.sum(w * den_c, axis=0, keepdims=True)))
    table = jnp.concatenate(
        [stats[0][0], stats[1][0], stats[0][1], stats[1][1], stats[0][2], stats[1][2],
         jnp.zeros((124 - 2 * n, 128), F32)],
        axis=0,
    )
    table = jnp.transpose(table)[:chunk]
    t2v = jnp.zeros((2 * n * 16, HEAD + 128), F32)
    sr, sc = iota((2 * n * 16, chunk), 0), iota((2 * n * 16, chunk), 1)
    for c in range(2):
        acc = jnp.zeros((chunk, HEAD), F32)
        for i in range(n):
            acc += rs_acc[i, :, c * HEAD:(c + 1) * HEAD].astype(F32) * spread(
                table[:, c * n + i:c * n + i + 1]
            )
        cols = split3(table[:, 2 * n + c:2 * n + c + 1]) + split3(table[:, 2 * n + 2 + c:2 * n + 3 + c])
        tile = jnp.zeros((chunk, 128), F32)
        for i, col in enumerate(cols):
            tile = jnp.where(lane_c == i, col, tile)
        rowsrc = jnp.concatenate([acc, tile], axis=1).astype(BF16)
        inner = lax.rem(sr, 16) - c * 8
        pick_rows = (inner >= 0) & (inner < reqs) & (lax.div(sr, 16) * reqs + inner == sc)
        t2v += dot(jnp.where(pick_rows, 1.0, 0.0).astype(BF16), rowsrc)
    t2[...] = t2v.astype(BF16).reshape(2 * n, 16, HEAD + 128)

    def home(pos, kk):
        return remote(
            t2.at[pos * 2 + kk], r2.at[k, p1], t2_send.at[pos * 2 + kk], t2_recv.at[k, p1],
            mine1(pos, kk),
        )

    for d in far[::-1]:
        pos = lax.rem(p1 + d, n)
        for kk in range(2):
            home(pos, kk).start()
    home(p1, other).start()
    r2[k, p1] = t2[p1 * 2 + k]
    loads[2].wait()
    for d in range(1, n):
        for h in range(2):
            src = lax.rem((y, z)[h] + d, n)
            remote(t2.at[0], r2.at[h, src], t2_send.at[0], t2_recv.at[h, src], partner).wait_recv()
    src = y + other * (z - y)
    remote(t2.at[0], r2.at[other, src], t2_send.at[0], t2_recv.at[other, src], partner).wait_recv()

    heads = []
    for h in range(2):
        cells = [r2[h, i].astype(F32) for i in range(n)]
        ms = [t[:, HEAD:HEAD + 1] + t[:, HEAD + 1:HEAD + 2] + t[:, HEAD + 2:HEAD + 3] for t in cells]
        ds = [t[:, HEAD + 3:HEAD + 4] + t[:, HEAD + 4:HEAD + 5] + t[:, HEAD + 5:HEAD + 6] for t in cells]
        ms.append(own_st[h * 16:(h + 1) * 16, 0:1])
        ds.append(own_st[h * 16:(h + 1) * 16, 1:2])
        accs = [t[:, :HEAD] for t in cells] + [own_acc[h * 16:(h + 1) * 16]]
        mx = functools.reduce(jnp.maximum, ms)
        num = jnp.zeros((16, HEAD), F32)
        dn = jnp.zeros((16, 1), F32)
        for m, dd, acc in zip(ms, ds, accs):
            w = jnp.exp(m - mx)
            num += acc * w
            dn += dd * w
        heads.append(num / dn)
    att = jnp.concatenate(
        [jnp.concatenate([a[0:8], a[8:16]], axis=1) for a in heads], axis=0
    ).astype(BF16)

    ar[x] = dot(att, wv[...]).astype(BF16)

    def share(d):
        return remote(
            ar.at[x], ar.at[x], ar_send.at[d], ar_recv.at[x], (lax.rem(x + d, nx), b)
        )

    for d in range(1, nx):
        share(d).start()
    for d in range(1, nx):
        src = lax.rem(x + nx - d, nx)
        remote(ar.at[src], ar.at[src], ar_send.at[d], ar_recv.at[src], partner).wait_recv()
    total = ar[0].astype(F32)
    for i in range(1, nx):
        total += ar[i].astype(F32)
    hid = (hid_ref[...].astype(F32) + total).astype(BF16)
    out_ref[...] = hid
    last = hid[8:16].astype(F32)
    normed = last * lax.rsqrt(jnp.mean(last * last, axis=1, keepdims=True) + 1e-06) * gain_ref[...]
    sc_ref[...] = jnp.broadcast_to(jnp.sum(normed * score_ref[...], axis=1, keepdims=True), (8, 128))

    for h in range(2):
        for d in range(1, n):
            first(h, d).wait_send()
    remote(q_ref.at[other], s1.at[remote_slot(n, y, z, k)], s1_send.at[other * n],
           s1_recv.at[remote_slot(n, y, z, k)], partner).wait_send()
    for d in far:
        second(lax.rem(p2 + d, n), p2).wait_send()
    for p in range(n):
        forward(p).wait_send()
        remote(xo_acc.at[p], rx_acc.at[p], xo_send.at[p], xo_recv.at[p], partner).wait_send()
        remote(xo_st.at[p], rx_st.at[p], xs_send.at[p], xs_recv.at[p], partner).wait_send()
    for d in far:
        to_ring_acc(lax.rem(p2 + d, n)).wait_send()
        to_ring_ml(lax.rem(p2 + d, n)).wait_send()
    for d in range(1, n):
        for kk in range(2):
            home(lax.rem(p1 + d, n), kk).wait_send()
    home(p1, other).wait_send()
    for d in range(1, nx):
        share(d).wait_send()


def remote_slot(n, y, z, k):
    return (z + k * (y - z)) * 2 + k


def rows_of(a):
    r = a.shape[0]
    a = a.reshape(r, 2, 2, HEAD).transpose(1, 2, 0, 3)
    return jnp.pad(a, ((0, 0), (0, 0), (0, 8 - r), (0, 0))).reshape(2, 16, HEAD)


def body(n, nx, prefix_pool, slot_page, prompt_len, request_ids, tail_len, tail_cache, queries,
         new_kv, hidden, out_weight, norm_gain, score_weight):
    pages = prefix_pool.shape[1]
    reqs, width = hidden.shape[0], hidden.shape[2]
    chunk = n * 2 * reqs
    rows = pages * SAMPLES
    total = n * chunk
    grid = request_ids.astype(F32).reshape(n, n, 2 * reqs)
    ids = jnp.stack([grid.reshape(n, chunk), grid.transpose(1, 0, 2).reshape(n, chunk)])
    ids = jnp.pad(ids, ((0, 0), (0, 0), (0, 128 - chunk)), constant_values=-1.0)
    q = rows_of(queries)
    nk = jnp.pad(new_kv[0].transpose(1, 0, 2), ((0, 0), (0, 8 - reqs), (0, 0))).reshape(16, 2 * HEAD)
    hid = jnp.pad(hidden.transpose(1, 0, 2), ((0, 0), (0, 8 - reqs), (0, 0))).reshape(16, width)
    vm = pl.BlockSpec(memory_space=pltpu.VMEM)
    sm = pl.BlockSpec(memory_space=pltpu.SMEM)
    hbm = pl.BlockSpec(memory_space=pl.ANY)
    dma = pltpu.SemaphoreType.DMA
    out, sc = pl.pallas_call(
        functools.partial(kernel, n, nx, reqs, pages),
        out_shape=(
            jax.ShapeDtypeStruct((16, width), BF16),
            jax.ShapeDtypeStruct((8, 128), F32),
        ),
        in_specs=[sm, sm, sm, vm, vm, vm, vm, vm, vm, hbm, hbm, hbm],
        out_specs=(vm, vm),
        scratch_shapes=[
            pltpu.VMEM((pages, PAGE, 2 * HEAD), BF16),
            pltpu.VMEM((reqs, 128, 2 * HEAD), BF16),
            pltpu.VMEM((2 * HEAD, width), BF16),
            pltpu.VMEM((2 * n, 16, HEAD), BF16),
            pltpu.VMEM((n, chunk, 512), BF16),
            pltpu.VMEM((n, chunk, 512), BF16),
            pltpu.VMEM((n, rows, chunk), BF16),
            pltpu.VMEM((n, rows, chunk), BF16),
            pltpu.VMEM((total, rows), BF16),
            pltpu.VMEM((total, rows), BF16),
            pltpu.VMEM((2, rows, 512), F32),
            pltpu.VMEM((2, rows, 512), BF16),
            pltpu.VMEM((2, rows, 384), BF16),
            pltpu.VMEM((n, chunk, 512), BF16),
            pltpu.VMEM((n, chunk, 128), F32),
            pltpu.VMEM((n, chunk, 512), BF16),
            pltpu.VMEM((n, chunk, 128), F32),
            pltpu.VMEM((n, chunk, 512), BF16),
            pltpu.VMEM((n, 8, 128), F32),
            pltpu.VMEM((n, chunk, 512), BF16),
            pltpu.VMEM((n, 8, 128), F32),
            pltpu.VMEM((2 * n, 16, HEAD + 128), BF16),
            pltpu.VMEM((2, n, 16, HEAD + 128), BF16),
            pltpu.VMEM((32, HEAD), F32),
            pltpu.VMEM((32, 128), F32),
            pltpu.VMEM((8, 128), F32),
            pltpu.VMEM((nx, 16, width), BF16),
            dma((3,)), dma((2 * n,)), dma((2 * n,)),
            dma((n,)), dma((n,)), dma((n,)), dma((n,)),
            dma((n,)), dma((n,)), dma((n,)), dma((n,)),
            dma((n,)), dma((n,)), dma((n,)), dma((n,)),
            dma((2 * n,)), dma((2, n)), dma((nx,)), dma((nx,)),
        ],
        compiler_params=pltpu.CompilerParams(collective_id=0, has_side_effects=True),
    )(
        slot_page, prompt_len, tail_len, ids, q, nk, hid, norm_gain.reshape(1, -1),
        score_weight.reshape(1, -1), prefix_pool[0], tail_cache[0], out_weight,
    )
    hidden_out = out.reshape(2, 8, width)[:, :reqs].transpose(1, 0, 2)
    return hidden_out, sc[:reqs, 0]


def solution(mesh):
    nx = mesh.shape["kv"]
    n = int(round((mesh.shape["blk"] // 2) ** 0.5))
    in_specs = (
        P("kv", "blk", None, None),
        P("blk"),
        P(),
        P(),
        P("blk"),
        P("kv", "blk", None, None),
        P("blk", None, "kv"),
        P("kv", "blk", None, None),
        P("blk", None, None),
        P("kv", None),
        P(),
        P(),
    )
    out_specs = (P("blk", None, None), P("blk"))
    return jax.shard_map(
        functools.partial(body, n, nx), mesh=mesh, in_specs=in_specs, out_specs=out_specs, check_vma=False
    )
```

time: 1180 us -> 76.2 us (0.06)
  blocking collectives: 994 us -> 0 us
  waiting for transfers between devices: 81.5 us -> 0 us
  Pallas kernels: 0 us -> 66.6 us
  other arithmetic: 52.7 us -> 1.29 us
  between operations: 14.3 us -> 0.66 us
  local copies, waits for them, and re-layouts: 20.6 us -> 7.17 us
    psum x2 -> x0, blocking collectives: 505 us -> none  [the longest x1 491 us: body(): total_num, total_den = lax.psum((prefix_num, prefix_den), 'blk')]
    pmax x1 -> x0, blocking collectives: 489 us -> none  [body(): global_peak = lax.pmax(local_peak, 'blk')]
    all_gather x1 -> x0, waiting for transfers between devices: 80.7 us -> none  [body(): all_queries = lax.all_gather(queries, 'blk', axis=0, tiled=True)]
    pallas_call x0 -> x1, Pallas kernels: none -> 66.6 us  [body(): pl.pallas_call(functools.partial(kernel, n, nx, reqs, pages), out_shape=(...]
    scatter-add x2 -> x0, other arithmetic: 45.4 us -> none  [the longest x1 43.5 us: page_sums(): jnp.zeros((total_count, row_count, head_size), jnp.float32).at[flat_rows]]
  transfers between devices with their start and end apart: 2 -> 0, of which waited for: 1 -> 0; matrix products, arithmetic and copies ran while one was open for 1% -> 0% of each run, Pallas kernels for 0% -> 0%
where the time goes in v1:
time: 76.2 us; the launch traced here: 75.8 us
  Pallas kernels  66.6 us (87%)
  local copies, waits for them, and re-layouts  7.17 us (9%)
  other arithmetic  1.29 us (2%)
    pallas_call x1, Pallas kernels, body(): pl.pallas_call(functools.partial(kernel, n, nx, reqs, pages), out_shape=(...  66.6 us
    unnamed x3, local copies, waits for them, and re-layouts  3.04 us

profile of v1, /device:TPU:1, one launch (start us, length us, event | category | flops | bytes accessed | tf_op | source)
XLA Modules:
  0.0 75.8 jit_solution(10362476817288552150)
XLA Ops:
  0.6 0.7 convert_element_type.9
  1.3 0.1 stack_reshape_reshape.3
  1.4 0.7 reshape.29
  2.1 0.6 pad_bitcast_fusion.2.q_ref
  2.7 0.7 copy.24
  3.5 0.6 pad_bitcast_fusion.1.nk_ref
  4.1 0.1 reshape.28
  4.2 0.1 stack_reshape.3
  4.3 0.6 select_maximum_fusion.ids_ref
  4.9 0.8 %copy.25 = bf16[2,6,2048]{2,1,0:T(8,128)(2,1)S(1)} copy(bf16[2,6,2048]{2,0,1:T(2,128)(2,1)} %bitcast.28) | data formatting | bytes 98304
  5.7 0.6 pad_bitcast_fusion.hid_ref
  6.3 66.6 %shard_map.131 = (bf16[16,2048]{1,0:T(8,128)(2,1)}, f32[8,128]{1,0:T(8,128)}) custom-call(s32[24]{0:T(128)} %slot_ref.1, s32[48]{0:T(128)} %plen_ref.1, s32[6]{0:T(128)} %tlen_ref.1, f32[2,8,128]{2,1,0:T(8,128)} %select_maximum_fusion.ids_ref, bf16[2,16,256]{2,1,0:T(8,128)(2,1)} %pad_bitcast_fusion.2.q_ref, bf16[16,512]{1,0:T(8,128)(2,1)} %pad_bitcast_fusion.1.nk_ref, ...), custom_call_target="tpu_custom_call" | custom-call | tf_op jit(solution)/shard_map/pallas_call | solution.py:483
  73.0 1.5 %copy.28 = bf16[2,6,2048]{2,0,1:T(2,128)(2,1)} copy(bf16[2,6,2048]{2,1,0:T(8,128)(2,1)} %bitcast.26) | data formatting | bytes 98304
  74.5 1.3 %slice_reduce_fusion = f32[6]{0:T(128)} fusion(f32[8,128]{1,0:T(8,128)} %get-tuple-element.5), kind=kLoop, calls=%fused_computation.7 | loop fusion | bytes 48 | tf_op jit(solution)/shard_map/slice | solution.py:531
  (2 shorter events, 0.0 us)

commit v2 on v1

v2 whole, which is shorter than its diff:
```python
import functools

import jax
import jax.numpy as jnp
from jax import lax
from jax.experimental import pallas as pl
from jax.experimental.pallas import tpu as pltpu
from jax.sharding import PartitionSpec as P

MESH = pl.DeviceIdType.MESH
SAMPLES = 16
HEAD = 256
PAGE = 64
NEG = -1e30
F32 = jnp.float32
BF16 = jnp.bfloat16


def iota(shape, dim):
    return lax.broadcasted_iota(jnp.int32, shape, dim)


def dot(a, b, ca=1, cb=0):
    return lax.dot_general(a, b, (((ca,), (cb,)), ((), ())), preferred_element_type=F32)


def floor_div(a, c):
    return jnp.floor((a.astype(F32) + 0.5) * (1.0 / c))


def split3(x):
    a = x.astype(BF16).astype(F32)
    b = (x - a).astype(BF16).astype(F32)
    return a, b, x - a - b


def kernel(
    n, nx, reqs, pages,
    slot_ref, plen_ref, tlen_ref, ids_ref, q_in, nk_ref, hid_ref, gain_ref, score_ref,
    pool_hbm, tail_hbm, w_hbm,
    out_ref, sc_ref,
    q_ref, poolv, tailv, wv, s1, agm, ago, gm, go, gt, pick, accm, acco, stats, ptgt, peak_tx, peak_rx, den_tx, den_rx,
    tx_acc, tx_ml, a3_acc, a4_acc, b_acc, rx_ml, t2, r2, own_acc, own_st, ar,
    local_sem, s1_send, s1_recv, ag_send, ag_recv, fw_send, fw_recv,
    cx_send, cx_recv, rs_send, rs_recv, rm_send, rm_recv,
    t2_send, t2_recv, ar_send, ar_recv,
):
    chunk = n * 2 * reqs
    half = chunk // 2
    rows = pages * SAMPLES
    prompts = plen_ref.shape[0]
    scale = HEAD ** (-0.5)
    x = lax.axis_index("kv")
    b = lax.axis_index("blk")
    k = lax.rem(b, 2)
    y = lax.rem(lax.div(b, 2), n)
    z = lax.div(b, 2 * n)
    p1 = y + k * (z - y)
    p2 = z + k * (y - z)
    other = 1 - k

    def at(zz, yy, kk):
        return (x, (zz * n + yy) * 2 + kk)

    def ring1(pos, h, kk):
        if h == 0:
            return at(z, pos, kk)
        return at(pos, y, kk)

    def mine1(pos, kk):
        return at(z + k * (pos - z), pos + k * (y - pos), kk)

    def mine2(d):
        pos = lax.rem(p2 + (d + n), n)
        return at(pos + k * (z - pos), y + k * (pos - y), k)

    def near(d):
        return lax.rem(p2 + (d + n), n)

    partner = at(z, y, other)

    def remote(src, dst, send, recv, to):
        return pltpu.make_async_remote_copy(
            src_ref=src, dst_ref=dst, send_sem=send, recv_sem=recv, device_id=to, device_id_type=MESH
        )

    pending = []

    def start(copy):
        copy.start()
        pending.append(copy)

    barrier = pltpu.get_barrier_semaphore()

    def greet(to):
        pl.semaphore_signal(barrier, inc=1, device_id=to, device_id_type=MESH)

    for d in [i for j in range(1, n // 2 + 1) for i in ((j, n - j) if 2 * j != n else (j,))]:
        for kk in range(2):
            greet(at(z, lax.rem(y + d, n), kk))
            greet(at(lax.rem(z + d, n), y, kk))
    greet(partner)
    for d in range(1, nx):
        greet((lax.rem(x + d, nx), b))

    loads = [
        pltpu.make_async_copy(pool_hbm, poolv, local_sem.at[0]),
        pltpu.make_async_copy(tail_hbm, tailv, local_sem.at[1]),
        pltpu.make_async_copy(w_hbm, wv, local_sem.at[2]),
    ]
    for load in loads:
        load.start()

    raw = q_in[...].astype(F32)
    gap = jnp.zeros((8 - reqs, HEAD), F32)
    for i in range(2):
        q_ref[i] = jnp.concatenate(
            [raw[:, i, 0:HEAD], gap, raw[:, i, HEAD:2 * HEAD], gap], axis=0
        ).astype(BF16)
    s1[p1 * 2 + k] = q_ref[k]

    pl.semaphore_wait(barrier, 1 + 4 * (n - 1) + (nx - 1))

    def first(h, d):
        mypos = (y, z)[h]
        pos = lax.rem(mypos + d, n)
        slot = mypos * 2 + k
        return remote(
            q_ref.at[h], s1.at[slot], s1_send.at[h * n + d], s1_recv.at[slot], ring1(pos, h, h)
        )

    order = [d for i in range(n // 2, 0, -1) for d in ((i, n - i) if 2 * i != n else (i,))]
    for d in order:
        for h in range(2):
            start(first(h, d))
    slot = p1_of(y, z, other) * 2 + k
    start(remote(q_ref.at[other], s1.at[slot], s1_send.at[other * n], s1_recv.at[slot], partner))

    lane = iota((1, 128), 1)
    lens = jnp.zeros((1, 128), jnp.int32)
    for p in range(prompts):
        lens = jnp.where(lane == p, plen_ref[p], lens)
    need = lax.shift_right_logical(lens + (PAGE - 1), 6).astype(F32)
    grid_r, grid_c = iota((128, 128), 0), iota((128, 128), 1)
    need_t = jnp.transpose(jnp.broadcast_to(need, (128, 128)))
    ends = jnp.sum(jnp.where(grid_r <= grid_c, need_t, 0.0), axis=0, keepdims=True)
    starts = ends - need
    page_r = iota((pages, 128), 0)
    slots = jnp.zeros((pages, 128), jnp.int32)
    for j in range(pages):
        slots = jnp.where(page_r == j, slot_ref[j], slots)
    slots = slots.astype(F32)
    plane = iota((pages, 128), 1)
    owner = jnp.sum(
        jnp.where((plane < prompts) & (slots >= ends), 1.0, 0.0), axis=1, keepdims=True
    )
    used = owner < prompts
    owner = jnp.minimum(owner, prompts - 1.0)
    mine = plane.astype(F32) == owner
    begin = jnp.sum(jnp.where(mine, starts, 0.0), axis=1, keepdims=True)
    length = jnp.sum(jnp.where(mine, lens.astype(F32), 0.0), axis=1, keepdims=True)
    live = jnp.where(used, length - (slots - begin) * PAGE, 0.0)
    sample = (iota((rows, 128), 0) & (SAMPLES - 1)).astype(F32)
    target = (
        jnp.broadcast_to((owner * SAMPLES + jnp.zeros_like(slots))[:, None, :], (pages, SAMPLES, 128))
        .reshape(rows, 128) + sample
    )
    live_c = jnp.broadcast_to(live[:, None, :], (pages, SAMPLES, 128)).reshape(rows, 128)
    target_row = jnp.concatenate(
        [jnp.transpose(target[i * 128:(i + 1) * 128])[0:8] for i in range(rows // 128)], axis=1
    )
    live_row = jnp.concatenate(
        [jnp.transpose(live_c[i * 128:(i + 1) * 128])[0:1] for i in range(rows // 128)], axis=1
    )
    ptgt[0] = target_row

    pr, pc = iota((chunk, 2 * n * 16), 0), iota((chunk, 2 * n * 16), 1).astype(F32)
    cell = floor_div(pr, reqs)
    want = cell * 16.0 + (pr.astype(F32) - cell * reqs)
    for d in range(n):
        for kk in range(2):
            slot = lax.rem(p1 + d, n) * 2 + lax.rem(k + kk, 2)
            if d or kk:
                remote(q_ref.at[0], s1.at[slot], s1_send.at[0], s1_recv.at[slot], partner).wait_recv()
    s1v = s1[...].reshape(2 * n * 16, HEAD)
    packed = [
        dot(jnp.where(pc == want + c * 8.0, 1.0, 0.0).astype(BF16), s1v) for c in range(2)
    ]
    agm[p2] = jnp.concatenate(packed, axis=1).astype(BF16)
    start(remote(ptgt.at[0], ptgt.at[1], cx_send.at[0], cx_recv.at[0], partner))

    def part(src, piece):
        return agm.at[src, pl.ds(piece * half, half)]

    def second(src, s, hop, kind, piece):
        return remote(
            part(src, piece), part(src, piece), ag_send.at[s, kind, piece], ag_recv.at[s, kind, piece],
            mine2((1, -1)[s] * hop),
        )

    def arrived(s, kind, piece):
        src = near(-(1, -1)[s] * (kind + 1))
        second(src, s, 1, kind, piece).wait_recv()
        return src

    def forward(src, piece):
        return remote(
            part(src, piece), ago.at[src, pl.ds(piece * half, half)], fw_send.at[src, piece],
            fw_recv.at[src, piece], partner,
        )

    for i in range(2):
        for s in range(2):
            start(second(p2, s, 2, 1, i ^ s))
    for i in range(2):
        for s in range(2):
            start(second(p2, s, 1, 0, i ^ s))
    for i in range(2):
        start(forward(p2, i))

    total = n * chunk
    ids = ids_ref[...]
    grid_u = iota((n * n, total), 0).astype(F32)
    grid_e = iota((n * n, total), 1)
    on = floor_div(grid_e, 2 * reqs) == grid_u
    e_in = iota((total, 128), 0)
    e_mod = e_in.astype(F32) - floor_div(e_in, 2 * reqs) * (2 * reqs)
    l_in = iota((1, 128), 1)
    l_div = floor_div(l_in, 2 * reqs)
    l_mod = l_in.astype(F32) - l_div * (2 * reqs)
    spread_e = jnp.where(e_mod == l_mod, 1.0, 0.0).astype(BF16)
    hi = jnp.where(on, lax.shift_right_logical(ids, 5).astype(F32), 0.0).astype(BF16)
    lo = jnp.where(on, (ids & 31).astype(F32), 0.0).astype(BF16)
    table = dot(hi, spread_e) * 32.0 + dot(lo, spread_e)
    nat = jnp.concatenate(
        [
            jnp.sum(
                jnp.where(iota((n, 128), 0).astype(F32) == l_div, table[i * n:(i + 1) * n], 0.0),
                axis=0, keepdims=True,
            )
            for i in range(n)
        ],
        axis=0,
    )
    perm = jnp.zeros((n, 128), F32)
    for i in range(n):
        perm = jnp.where(l_div == float(i), table[i * n:(i + 1) * n], perm)
    ids_m = jnp.where(k == 0, nat, perm)
    ids_o = jnp.where(k == 0, perm, nat)
    for p in range(n):
        gm[p] = jnp.where(target[:, :chunk] == ids_m[p:p + 1, :chunk], 1.0, 0.0).astype(BF16)

    for i in range(2):
        for s in range(2):
            piece = i ^ s
            src = arrived(s, 1, piece)
            if i == 0:
                start(second(src, s, 2, 3, piece))
            start(second(src, s, 1, 2, piece))
            start(forward(src, piece))
    pick[0] = dot(gm[p2], agm[p2])
    for i in range(2):
        for s in range(2):
            piece = i ^ s
            start(forward(arrived(s, 0, piece), piece))
    for p in range(n):
        go[p] = jnp.where(target[:, :chunk] == ids_o[p:p + 1, :chunk], 1.0, 0.0).astype(BF16)
    for s in range(2):
        for dd in (2, 1):
            src = near(-(1, -1)[s] * dd)
            pick[0] += dot(gm[src], agm[src])

    def from_core(pos, first_one=False):
        for piece in range(2):
            forward(pos, piece).wait_recv()
        got = dot(go[pos], ago[pos])
        pick[1] = got if first_one else pick[1] + got

    from_core(p1, True)
    for dd in (2, -2, 1, -1):
        from_core(lax.rem(p1 + dd + n, n))
    for i in range(2):
        for s in range(2):
            piece = i ^ s
            start(forward(arrived(s, 2, piece), piece))
    for s in range(2):
        src = near(-(1, -1)[s] * 3)
        pick[0] += dot(gm[src], agm[src])
    for s in range(2):
        start(forward(arrived(s, 3, s), s))
    src = near(4)
    pick[0] += dot(gm[src], agm[src])
    for dd in (3, -3, 4):
        from_core(lax.rem(p1 + dd + n, n))

    loads[0].wait()
    blocks = pages // 8
    scores, peaks = [], []
    page_l = lax.shift_right_logical(iota((PAGE, 512), 1) & 127, 4)
    for blk in range(blocks):
        keys = poolv[blk * 8:(blk + 1) * 8].reshape(8 * PAGE, 2 * HEAD)[:, :HEAD]
        qb = jnp.concatenate(
            [
                pick[h, blk * 128:(blk + 1) * 128, c * HEAD:(c + 1) * HEAD].astype(BF16)
                for h in range(2) for c in range(2)
            ],
            axis=0,
        )
        full = dot(keys, qb, 1, 1)
        s = jnp.zeros((PAGE, 512), F32)
        for j in range(8):
            s = jnp.where(page_l == j, full[j * PAGE:(j + 1) * PAGE], s)
        lv = jnp.concatenate([live_row[:, blk * 128:(blk + 1) * 128]] * 4, axis=1)
        alive = iota((PAGE, 512), 0).astype(F32) < lv
        s = jnp.where(alive, s * scale, NEG)
        scores.append((s, alive))
        m = jnp.max(s, axis=0, keepdims=True)
        peaks.append(jnp.concatenate([m[:, i * 128:(i + 1) * 128] for i in range(4)], axis=0))
    local = jnp.concatenate(peaks, axis=1)
    peak_tx[...] = jnp.concatenate([local[2:4], local[0:2], local], axis=0)
    start(remote(peak_tx, peak_rx, cx_send.at[1], cx_recv.at[1], partner))

    remote(ptgt.at[0], ptgt.at[1], cx_send.at[0], cx_recv.at[0], partner).wait_recv()
    tgt_p = ptgt[1]
    both_t = jnp.concatenate([target_row[0:4], tgt_p[0:4]], axis=0)
    swap_t = jnp.concatenate([tgt_p[0:4], target_row[0:4]], axis=0)
    lane8 = iota((8, rows), 1)
    lower = iota((8, rows), 0) >= 4
    lead = jnp.where(lower & (swap_t == both_t), 0.0, 1.0)
    for d in range(1, pages):
        same = pltpu.roll(both_t, d * SAMPLES, 1) == both_t
        cross = pltpu.roll(swap_t, d * SAMPLES, 1) == both_t
        lead = jnp.where((same & (lane8 >= d * SAMPLES)) | (cross & lower), 0.0, lead)
    remote(peak_tx, peak_rx, cx_send.at[1], cx_recv.at[1], partner).wait_recv()
    peer = peak_rx[...]
    both_m = jnp.concatenate([local, peer[0:4]], axis=0)
    swap_m = jnp.concatenate([peer[0:4], local], axis=0)
    top = jnp.where(swap_t == both_t, jnp.maximum(both_m, swap_m), both_m)
    for d in range(1, pages):
        same = pltpu.roll(both_t, d * SAMPLES, 1) == both_t
        cross = pltpu.roll(swap_t, d * SAMPLES, 1) == both_t
        top = jnp.where(same, jnp.maximum(top, pltpu.roll(both_m, d * SAMPLES, 1)), top)
        top = jnp.where(cross, jnp.maximum(top, pltpu.roll(swap_m, d * SAMPLES, 1)), top)

    def give(blk):
        sl = pl.ds(blk * 128, 128)
        return remote(
            acco.at[sl], accm.at[pl.ds(rows + blk * 128, 128)], cx_send.at[3 + blk], cx_recv.at[3 + blk],
            partner,
        )

    dens = []
    for blk in range(blocks):
        s, alive = scores[blk]
        tb = top[:, blk * 128:(blk + 1) * 128]
        tb = jnp.concatenate([tb[i:i + 1] for i in range(4)], axis=1)
        w = jnp.where(alive, jnp.exp(s - tb), 0.0)
        dsum = jnp.sum(w, axis=0, keepdims=True)
        dens.append(jnp.concatenate([dsum[:, i * 128:(i + 1) * 128] for i in range(4)], axis=0))
        wide = jnp.concatenate([jnp.where(page_l == j, w, 0.0) for j in range(8)], axis=0)
        values = poolv[blk * 8:(blk + 1) * 8].reshape(8 * PAGE, 2 * HEAD)[:, HEAD:]
        acc = dot(jnp.transpose(wide).astype(BF16), values)
        for c in range(2):
            acco[blk * 128:(blk + 1) * 128, c * HEAD:(c + 1) * HEAD] = (
                acc[(2 + c) * 128:(3 + c) * 128].astype(BF16)
            )
        start(give(blk))
        for c in range(2):
            accm[blk * 128:(blk + 1) * 128, c * HEAD:(c + 1) * HEAD] = (
                acc[c * 128:(c + 1) * 128].astype(BF16)
            )
    den = jnp.concatenate(dens, axis=1)
    den_tx[...] = jnp.concatenate([den[2:4], den[2:4], den], axis=0)
    start(remote(den_tx, den_rx, cx_send.at[2], cx_recv.at[2], partner))
    for p in range(n):
        if p == 0:
            ids_t = jnp.transpose(jnp.concatenate([ids_m, jnp.zeros((128 - n, 128), F32)], axis=0))
            all_t = jnp.concatenate([target_row[0:1], tgt_p[0:1]], axis=1)
        gt[pl.ds(p * chunk, chunk), :] = jnp.where(ids_t[:chunk, p:p + 1] == all_t, 1.0, 0.0).astype(BF16)
    remote(den_tx, den_rx, cx_send.at[2], cx_recv.at[2], partner).wait_recv()
    den_p = den_rx[...]
    st = jnp.concatenate(
        [
            jnp.concatenate([jnp.where(lead[0:2] > 0.5, top[0:2], 0.0),
                             jnp.where(lead[4:6] > 0.5, top[4:6], 0.0)], axis=1),
            jnp.concatenate([den[0:2], den_p[0:2]], axis=1),
            jnp.concatenate([lead[0:1], lead[4:5]], axis=1),
            jnp.zeros((3, 2 * rows), F32),
        ],
        axis=0,
    )
    stats[...] = jnp.concatenate(split3(st), axis=0).astype(BF16)
    for blk in range(blocks):
        give(blk).wait_recv()

    sub8 = iota((8, 128), 0)

    def sums(d):
        g = gt[pl.ds(pl.multiple_of(near(d) * chunk, chunk), chunk), :]
        acc = dot(g, accm[...])
        ml = dot(stats[...], g, 1, 1)
        ml = ml[0:8] + ml[8:16] + ml[16:24]
        ml = jnp.concatenate([ml, jnp.zeros((8, 128 - chunk), F32)], axis=1)
        return acc, jnp.where((sub8 < 2) & (ml[4:5] < 0.5), NEG, ml)

    def ring(s, kind, src, dst, hop):
        to = mine2((1, -1)[s] * hop)
        return (
            remote(src[0], dst, rs_send.at[s, kind], rs_recv.at[s, kind], to),
            remote(src[1], rx_ml.at[s, kind], rm_send.at[s, kind], rm_recv.at[s, kind], to),
        )

    def landed(s, kind, dst):
        for copy in ring(s, kind, (dst, rx_ml.at[s, kind]), dst, 1):
            copy.wait_recv()

    def store(i, d):
        acc, ml = sums(d)
        tx_acc[i] = acc.astype(BF16)
        tx_ml[i] = ml

    store(2, 4)
    for s in range(2):
        for copy in ring(s, 1, (tx_acc.at[2, pl.ds(s * half, half)], tx_ml.at[2]), a4_acc.at[s], 2):
            start(copy)
    for s in range(2):
        store(s, (3, -3)[s])
        for copy in ring(s, 0, (tx_acc.at[s], tx_ml.at[s]), a3_acc.at[s], 1):
            start(copy)
    for s in range(2):
        store(3 + s, (1, -1)[s])
        for copy in ring(s, 2, (tx_acc.at[3 + s], tx_ml.at[3 + s]), b_acc.at[s, 0], 1):
            start(copy)

    def weigh(mls):
        out = []
        for c in range(2):
            mx = functools.reduce(jnp.maximum, [m[c:c + 1] for m in mls])
            w = [jnp.exp(m[c:c + 1] - mx) for m in mls]
            dn = functools.reduce(jnp.add, [a * m[2 + c:3 + c] for a, m in zip(w, mls)])
            out.append((w, mx, dn))
        return out

    def columns(items):
        return jnp.transpose(
            jnp.concatenate(items + [jnp.zeros((128 - len(items), 128), F32)], axis=0)
        )

    lane128 = iota((8, 128), 1)
    for s in range(2):
        acc, ml = sums((2, -2)[s])
        landed(s, 0, a3_acc.at[s])
        landed(s, 1, a4_acc.at[s])
        inside = (lane128 < half) if s == 0 else (lane128 >= half)
        ml4 = jnp.where((sub8 < 2) & jnp.logical_not(inside), NEG, rx_ml[s, 1])
        mls = [ml, rx_ml[s, 0], ml4]
        st = weigh(mls)
        cols = columns(st[0][0] + st[1][0])
        outs = []
        for c in range(2):
            sl = slice(c * HEAD, (c + 1) * HEAD)
            a3 = a3_acc[s, :, sl].astype(F32)
            a4 = a4_acc[s, :, sl].astype(F32)
            v = acc[:, sl] * cols[:chunk, 3 * c:3 * c + 1] + a3 * cols[:chunk, 3 * c + 1:3 * c + 2]
            add = a4 * cols[s * half:(s + 1) * half, 3 * c + 2:3 * c + 3]
            if s == 0:
                v = jnp.concatenate([v[:half] + add, v[half:]], axis=0)
            else:
                v = jnp.concatenate([v[:half], v[half:] + add], axis=0)
            outs.append(v)
        tx_acc[5 + s] = jnp.concatenate(outs, axis=1).astype(BF16)
        tx_ml[5 + s] = jnp.concatenate(
            [st[0][1], st[1][1], st[0][2], st[1][2], jnp.zeros((4, 128), F32)], axis=0
        )
        for copy in ring(s, 3, (tx_acc.at[5 + s], tx_ml.at[5 + s]), b_acc.at[s, 1], 2):
            start(copy)
    home_acc, home_ml = sums(0)

    loads[1].wait()
    qown = jnp.concatenate([q_ref[0], q_ref[1]], axis=0)
    tails = tailv[...].reshape(reqs * 128, 2 * HEAD)
    row32 = iota((32, 128), 0) & 7
    ts, tl = [], []
    for r in range(reqs):
        ok = (row32 == r) & (iota((32, 128), 1) < tlen_ref[r])
        tl.append(ok)
        ts.append(jnp.where(ok, dot(qown, tails[r * 128:(r + 1) * 128, :HEAD], 1, 1) * scale, NEG))
    fresh = nk_ref[...].astype(F32)
    pad = jnp.zeros((8 - reqs, 2 * HEAD), F32)
    news = jnp.concatenate([fresh[:, 0, :], pad, fresh[:, 1, :], pad], axis=0).astype(BF16)
    nrow, ncol = iota((32, 16), 0), iota((32, 16), 1)
    nlive = ((nrow & 7) == (ncol & 7)) & (lax.shift_right_logical(ncol, 3) <= lax.shift_right_logical(nrow, 4))
    ns = jnp.where(nlive, dot(qown, news[:, :HEAD], 1, 1) * scale, NEG)
    peak = jnp.max(ns, axis=1, keepdims=True)
    peak = jnp.maximum(peak, jnp.max(functools.reduce(jnp.maximum, ts), axis=1, keepdims=True))
    nw = jnp.where(nlive, jnp.exp(ns - peak), 0.0)
    tw = [jnp.where(ok, jnp.exp(t - peak), 0.0) for t, ok in zip(ts, tl)]
    own_den = jnp.sum(nw, axis=1, keepdims=True)
    own_den += jnp.sum(functools.reduce(jnp.add, tw), axis=1, keepdims=True)
    own_acc[...] = dot(nw.astype(BF16), news[:, HEAD:]) + dot(
        jnp.concatenate(tw, axis=1).astype(BF16), tails[:, HEAD:]
    )
    own_st[...] = jnp.where(iota((32, 128), 1) == 0, peak, own_den)

    for s in range(2):
        landed(s, 2, b_acc.at[s, 0])
    for s in range(2):
        landed(s, 3, b_acc.at[s, 1])
    st = weigh([home_ml] + [rx_ml[s, kind] for s in range(2) for kind in (2, 3)])
    cols = columns(st[0][0] + st[1][0] + [st[0][1], st[1][1], st[0][2], st[1][2]])[:chunk]
    lane_c = iota((chunk, 128), 1)
    t2v = jnp.zeros((2 * n * 16, HEAD + 128), F32)
    sr, sc = iota((2 * n * 16, chunk), 0), iota((2 * n * 16, chunk), 1)
    for c in range(2):
        sl = slice(c * HEAD, (c + 1) * HEAD)
        acc = home_acc[:, sl] * cols[:, 5 * c:5 * c + 1]
        for i in range(4):
            acc += b_acc[i // 2, i % 2, :, sl].astype(F32) * cols[:, 5 * c + 1 + i:5 * c + 2 + i]
        parts = split3(cols[:, 10 + c:11 + c]) + split3(cols[:, 12 + c:13 + c])
        tile = jnp.zeros((chunk, 128), F32)
        for i, col in enumerate(parts):
            tile = jnp.where(lane_c == i, col, tile)
        rowsrc = jnp.concatenate([acc, tile], axis=1).astype(BF16)
        inner = (sr & 15) - c * 8
        pick_rows = (inner >= 0) & (inner < reqs) & (lax.shift_right_logical(sr, 4) * reqs + inner == sc)
        t2v += dot(jnp.where(pick_rows, 1.0, 0.0).astype(BF16), rowsrc)
    t2[...] = t2v.astype(BF16).reshape(2 * n, 16, HEAD + 128)

    def home(pos, kk):
        return remote(
            t2.at[pos * 2 + kk], r2.at[k, p1], t2_send.at[pos * 2 + kk], t2_recv.at[k, p1],
            mine1(pos, kk),
        )

    for d in order:
        pos = lax.rem(p1 + d, n)
        for kk in range(2):
            start(home(pos, kk))
    start(home(p1, other))
    r2[k, p1] = t2[p1 * 2 + k]
    loads[2].wait()
    for d in range(1, n):
        for h in range(2):
            src = lax.rem((y, z)[h] + d, n)
            remote(t2.at[0], r2.at[h, src], t2_send.at[0], t2_recv.at[h, src], partner).wait_recv()
    src = p1_of(y, z, other)
    remote(t2.at[0], r2.at[other, src], t2_send.at[0], t2_recv.at[other, src], partner).wait_recv()

    heads = []
    for h in range(2):
        cells = [r2[h, i].astype(F32) for i in range(n)]
        ms = [t[:, HEAD:HEAD + 1] + t[:, HEAD + 1:HEAD + 2] + t[:, HEAD + 2:HEAD + 3] for t in cells]
        ds = [t[:, HEAD + 3:HEAD + 4] + t[:, HEAD + 4:HEAD + 5] + t[:, HEAD + 5:HEAD + 6] for t in cells]
        ms.append(own_st[h * 16:(h + 1) * 16, 0:1])
        ds.append(own_st[h * 16:(h + 1) * 16, 1:2])
        accs = [t[:, :HEAD] for t in cells] + [own_acc[h * 16:(h + 1) * 16]]
        mx = functools.reduce(jnp.maximum, ms)
        num = jnp.zeros((16, HEAD), F32)
        dn = jnp.zeros((16, 1), F32)
        for m, dd, acc in zip(ms, ds, accs):
            w = jnp.exp(m - mx)
            num += acc * w
            dn += dd * w
        heads.append(num / dn)
    att = jnp.concatenate(
        [jnp.concatenate([a[0:8], a[8:16]], axis=1) for a in heads], axis=0
    ).astype(BF16)

    ar[x] = dot(att, wv[...]).astype(BF16)

    def share(d):
        return remote(
            ar.at[x], ar.at[x], ar_send.at[d], ar_recv.at[x], (lax.rem(x + d, nx), b)
        )

    for d in range(1, nx):
        start(share(d))
    raw_h = hid_ref[...].astype(F32)
    for d in range(1, nx):
        src = lax.rem(x + nx - d, nx)
        remote(ar.at[src], ar.at[src], ar_send.at[d], ar_recv.at[src], partner).wait_recv()
    total_h = ar[0].astype(F32)
    for i in range(1, nx):
        total_h += ar[i].astype(F32)
    hid = [(raw_h[:, i, :] + total_h[8 * i:8 * i + reqs]).astype(BF16).astype(F32) for i in range(2)]
    out_ref[...] = jnp.stack(hid, axis=1).astype(BF16)
    last = hid[1]
    normed = last * lax.rsqrt(jnp.mean(last * last, axis=1, keepdims=True) + 1e-06) * gain_ref[...]
    sc_ref[...] = jnp.broadcast_to(jnp.sum(normed * score_ref[...], axis=1, keepdims=True), (reqs, 128))
    for copy in pending:
        copy.wait_send()


def p1_of(y, z, h):
    return y + h * (z - y)


def body(n, nx, prefix_pool, slot_page, prompt_len, request_ids, tail_len, tail_cache, queries,
         new_kv, hidden, out_weight, norm_gain, score_weight):
    pages = prefix_pool.shape[1]
    reqs, width = hidden.shape[0], hidden.shape[2]
    chunk = n * 2 * reqs
    rows = pages * SAMPLES
    total = n * chunk
    vm = pl.BlockSpec(memory_space=pltpu.VMEM)
    sm = pl.BlockSpec(memory_space=pltpu.SMEM)
    hbm = pl.BlockSpec(memory_space=pl.ANY)
    dma = pltpu.SemaphoreType.DMA
    out, sc = pl.pallas_call(
        functools.partial(kernel, n, nx, reqs, pages),
        out_shape=(
            jax.ShapeDtypeStruct((reqs, 2, width), BF16),
            jax.ShapeDtypeStruct((reqs, 128), F32),
        ),
        in_specs=[sm, sm, sm, vm, vm, vm, vm, vm, vm, hbm, hbm, hbm],
        out_specs=(vm, vm),
        scratch_shapes=[
            pltpu.VMEM((2, 16, HEAD), BF16),
            pltpu.VMEM((pages, PAGE, 2 * HEAD), BF16),
            pltpu.VMEM((reqs, 128, 2 * HEAD), BF16),
            pltpu.VMEM((2 * HEAD, width), BF16),
            pltpu.VMEM((2 * n, 16, HEAD), BF16),
            pltpu.VMEM((n, chunk, 512), BF16),
            pltpu.VMEM((n, chunk, 512), BF16),
            pltpu.VMEM((n, rows, chunk), BF16),
            pltpu.VMEM((n, rows, chunk), BF16),
            pltpu.VMEM((total, 2 * rows), BF16),
            pltpu.VMEM((2, rows, 512), F32),
            pltpu.VMEM((2 * rows, 512), BF16),
            pltpu.VMEM((rows, 512), BF16),
            pltpu.VMEM((24, 2 * rows), BF16),
            pltpu.VMEM((2, 8, rows), F32),
            pltpu.VMEM((8, rows), F32),
            pltpu.VMEM((8, rows), F32),
            pltpu.VMEM((8, rows), F32),
            pltpu.VMEM((8, rows), F32),
            pltpu.VMEM((7, chunk, 512), BF16),
            pltpu.VMEM((7, 8, 128), F32),
            pltpu.VMEM((2, chunk, 512), BF16),
            pltpu.VMEM((2, chunk // 2, 512), BF16),
            pltpu.VMEM((2, 2, chunk, 512), BF16),
            pltpu.VMEM((2, 4, 8, 128), F32),
            pltpu.VMEM((2 * n, 16, HEAD + 128), BF16),
            pltpu.VMEM((2, n, 16, HEAD + 128), BF16),
            pltpu.VMEM((32, HEAD), F32),
            pltpu.VMEM((32, 128), F32),
            pltpu.VMEM((nx, 16, width), BF16),
            dma((3,)), dma((2 * n,)), dma((2 * n,)),
            dma((2, 4, 2)), dma((2, 4, 2)), dma((n, 2)), dma((n, 2)),
            dma((3 + pages // 8,)), dma((3 + pages // 8,)),
            dma((2, 4)), dma((2, 4)), dma((2, 4)), dma((2, 4)),
            dma((2 * n,)), dma((2, n)), dma((nx,)), dma((nx,)),
        ],
        compiler_params=pltpu.CompilerParams(collective_id=0, has_side_effects=True),
    )(
        slot_page, prompt_len, tail_len, request_ids.reshape(1, -1), queries, new_kv[0], hidden,
        norm_gain.reshape(1, -1), score_weight.reshape(1, -1), prefix_pool[0], tail_cache[0], out_weight,
    )
    return out, sc[:, 0]


def solution(mesh):
    nx = mesh.shape["kv"]
    n = int(round((mesh.shape["blk"] // 2) ** 0.5))
    in_specs = (
        P("kv", "blk", None, None),
        P("blk"),
        P(),
        P(),
        P("blk"),
        P("kv", "blk", None, None),
        P("blk", None, "kv"),
        P("kv", "blk", None, None),
        P("blk", None, None),
        P("kv", None),
        P(),
        P(),
    )
    out_specs = (P("blk", None, None), P("blk"))
    return jax.shard_map(
        functools.partial(body, n, nx), mesh=mesh, in_specs=in_specs, out_specs=out_specs, check_vma=False
    )
```

time: 76.2 us -> 65.8 us (0.86)
  Pallas kernels: 66.6 us -> 60.9 us
  local copies, waits for them, and re-layouts: 7.17 us -> 4.03 us
  other arithmetic: 1.29 us -> 0 us
    pallas_call x1, Pallas kernels: 66.6 us -> 60.9 us  [body(): pl.pallas_call(functools.partial(kernel, n, nx, reqs, pages), out_shape=(...]
    unnamed x3 -> x1, local copies, waits for them, and re-layouts: 3.04 us -> 1.45 us
    reshape x6 -> x1, local copies, waits for them, and re-layouts: 2.67 us -> 1.27 us  [body(): request_ids.reshape(1, -1)]
where the time goes in v2:
time: 65.8 us; the launch traced here: 65.5 us
  Pallas kernels  60.9 us (93%)
  local copies, waits for them, and re-layouts  4.03 us (6%)
    pallas_call x1, Pallas kernels, body(): pl.pallas_call(functools.partial(kernel, n, nx, reqs, pages), out_shape=(...  60.9 us
    unnamed x1, local copies, waits for them, and re-layouts  1.45 us

profile of v2, /device:TPU:1, one launch (start us, length us, event | category | flops | bytes accessed | tf_op | source)
XLA Modules:
  0.0 65.5 jit_solution(6887091916306082351)
XLA Ops:
  0.6 1.3 %reshape.13.ids_ref = s32[1,768]{1,0:T(1,128)} reshape(s32[768]{0:T(1024)} %param.15) | data formatting | bytes 6144 | tf_op jit(solution)/shard_map/reshape | solution.py:656
  1.9 60.9 %shard_map.131 = (bf16[6,2,2048]{2,1,0:T(2,128)(2,1)}, f32[6,128]{1,0:T(8,128)}) custom-call(s32[24]{0:T(128)} %slot_ref.1, s32[48]{0:T(128)} %plen_ref.1, s32[6]{0:T(128)} %tlen_ref.1, s32[1,768]{1,0:T(1,128)} %reshape.13.ids_ref, bf16[6,2,512]{2,1,0:T(2,128)(2,1)} %q_in.1, bf16[6,2,512]{2,1,0:T(2,128)(2,1)} %bitcast.7, bf16[6,2,2048]{2,1,0:T(2,128)(2,1)} %hid_ref.1, ...), custom_call_target="tpu_custom_call" | custom-call | tf_op jit(solution)/shard_map/pallas_call | solution.py:609
  62.8 1.3 %slice_reduce_fusion = f32[6]{0:T(128)} fusion(f32[6,128]{1,0:T(8,128)} %get-tuple-element.5), kind=kLoop, calls=%fused_computation | loop fusion | bytes 48 | tf_op jit(solution)/shard_map/slice | solution.py:659
  64.1 1.5 %copy.15 = bf16[6,2,2048]{2,1,0:T(2,128)(2,1)} copy(bf16[6,2,2048]{2,1,0:T(2,128)(2,1)} %get-tuple-element.8) | data formatting | bytes 98304

commit v3 on v2

--- a/solution.py
+++ b/solution.py
@@ -36,12 +36,12 @@
 
 def kernel(
     n, nx, reqs, pages,
-    slot_ref, plen_ref, tlen_ref, ids_ref, q_in, nk_ref, hid_ref, gain_ref, score_ref,
-    pool_hbm, tail_hbm, w_hbm,
-    out_ref, sc_ref,
-    q_ref, poolv, tailv, wv, s1, agm, ago, gm, go, gt, pick, accm, acco, stats, ptgt, peak_tx, peak_rx, den_tx, den_rx,
-    tx_acc, tx_ml, a3_acc, a4_acc, b_acc, rx_ml, t2, r2, own_acc, own_st, ar,
-    local_sem, s1_send, s1_recv, ag_send, ag_recv, fw_send, fw_recv,
+    slot_hbm, plen_hbm, tlen_hbm, ids_hbm, q_hbm, nk_hbm, pool_hbm, tail_hbm, w_hbm,
+    out_ref,
+    slot_ref, plen_ref, tlen_ref, ids_ref, q_in, nk_ref,
+    q_ref, poolv, tailv, wv, s1, agm, gm, gt, pick, accm, stats, info_tx, info_rx,
+    tx_acc, tx_ml, a3_acc, a4_acc, b_acc, rx_ml, t2, r2, own_acc, own_st, ar, ar_rx,
+    local_sem, s1_send, s1_recv, ag_send, ag_recv,
     cx_send, cx_recv, rs_send, rs_recv, rm_send, rm_recv,
     t2_send, t2_recv, ar_send, ar_recv,
 ):
@@ -100,16 +100,22 @@
             greet(at(z, lax.rem(y + d, n), kk))
             greet(at(lax.rem(z + d, n), y, kk))
     greet(partner)
-    for d in range(1, nx):
-        greet((lax.rem(x + d, nx), b))
+    if nx > 1:
+        greet((x + 1 - 2 * lax.rem(x, 2), b))
+    if nx > 2:
+        greet((nx - 1 - x, b))
 
     loads = [
-        pltpu.make_async_copy(pool_hbm, poolv, local_sem.at[0]),
-        pltpu.make_async_copy(tail_hbm, tailv, local_sem.at[1]),
-        pltpu.make_async_copy(w_hbm, wv, local_sem.at[2]),
+        pltpu.make_async_copy(src, dst, local_sem.at[i])
+        for i, (src, dst) in enumerate([
+            (q_hbm, q_in), (plen_hbm, plen_ref), (slot_hbm, slot_ref), (ids_hbm, ids_ref),
+            (pool_hbm, poolv.at[pl.ds(0, pages)]), (tlen_hbm, tlen_ref), (nk_hbm, nk_ref),
+            (tail_hbm, tailv), (w_hbm, wv),
+        ])
     ]
     for load in loads:
         load.start()
+    loads[0].wait()
 
     raw = q_in[...].astype(F32)
     gap = jnp.zeros((8 - reqs, HEAD), F32)
@@ -119,7 +125,7 @@
         ).astype(BF16)
     s1[p1 * 2 + k] = q_ref[k]
 
-    pl.semaphore_wait(barrier, 1 + 4 * (n - 1) + (nx - 1))
+    pl.semaphore_wait(barrier, 1 + 4 * (n - 1) + min(nx - 1, 2))
 
     def first(h, d):
         mypos = (y, z)[h]
@@ -136,6 +142,11 @@
     slot = p1_of(y, z, other) * 2 + k
     start(remote(q_ref.at[other], s1.at[slot], s1_send.at[other * n], s1_recv.at[slot], partner))
 
+    swap = remote(pool_hbm, poolv.at[pl.ds(pages, pages)], cx_send.at[0], cx_recv.at[0], partner)
+    start(swap)
+
+    loads[1].wait()
+    loads[2].wait()
     lane = iota((1, 128), 1)
     lens = jnp.zeros((1, 128), jnp.int32)
     for p in range(prompts):
@@ -160,19 +171,10 @@
     begin = jnp.sum(jnp.where(mine, starts, 0.0), axis=1, keepdims=True)
     length = jnp.sum(jnp.where(mine, lens.astype(F32), 0.0), axis=1, keepdims=True)
     live = jnp.where(used, length - (slots - begin) * PAGE, 0.0)
-    sample = (iota((rows, 128), 0) & (SAMPLES - 1)).astype(F32)
-    target = (
-        jnp.broadcast_to((owner * SAMPLES + jnp.zeros_like(slots))[:, None, :], (pages, SAMPLES, 128))
-        .reshape(rows, 128) + sample
-    )
-    live_c = jnp.broadcast_to(live[:, None, :], (pages, SAMPLES, 128)).reshape(rows, 128)
-    target_row = jnp.concatenate(
-        [jnp.transpose(target[i * 128:(i + 1) * 128])[0:8] for i in range(rows // 128)], axis=1
-    )
-    live_row = jnp.concatenate(
-        [jnp.transpose(live_c[i * 128:(i + 1) * 128])[0:1] for i in range(rows // 128)], axis=1
-    )
-    ptgt[0] = target_row
+    info_tx[0] = owner * SAMPLES + jnp.zeros_like(slots)
+    info_tx[1] = live + jnp.zeros_like(slots)
+    info = remote(info_tx, info_rx, cx_send.at[1], cx_recv.at[1], partner)
+    start(info)
 
     pr, pc = iota((chunk, 2 * n * 16), 0), iota((chunk, 2 * n * 16), 1).astype(F32)
     cell = floor_div(pr, reqs)
@@ -187,7 +189,6 @@
         dot(jnp.where(pc == want + c * 8.0, 1.0, 0.0).astype(BF16), s1v) for c in range(2)
     ]
     agm[p2] = jnp.concatenate(packed, axis=1).astype(BF16)
-    start(remote(ptgt.at[0], ptgt.at[1], cx_send.at[0], cx_recv.at[0], partner))
 
     def part(src, piece):
         return agm.at[src, pl.ds(piece * half, half)]
@@ -202,12 +203,6 @@
         src = near(-(1, -1)[s] * (kind + 1))
         second(src, s, 1, kind, piece).wait_recv()
         return src
-
-    def forward(src, piece):
-        return remote(
-            part(src, piece), ago.at[src, pl.ds(piece * half, half)], fw_send.at[src, piece],
-            fw_recv.at[src, piece], partner,
-        )
 
     for i in range(2):
         for s in range(2):
@@ -215,11 +210,10 @@
     for i in range(2):
         for s in range(2):
             start(second(p2, s, 1, 0, i ^ s))
-    for i in range(2):
-        start(forward(p2, i))
 
     total = n * chunk
-    ids = ids_ref[...]
+    loads[3].wait()
+    ids = ids_ref[...].reshape(1, total)
     grid_u = iota((n * n, total), 0).astype(F32)
     grid_e = iota((n * n, total), 1)
     on = floor_div(grid_e, 2 * reqs) == grid_u
@@ -246,7 +240,16 @@
     for i in range(n):
         perm = jnp.where(l_div == float(i), table[i * n:(i + 1) * n], perm)
     ids_m = jnp.where(k == 0, nat, perm)
-    ids_o = jnp.where(k == 0, perm, nat)
+    info.wait_recv()
+    pair = 2 * pages
+    sample = (iota((2 * rows, 128), 0) & (SAMPLES - 1)).astype(F32)
+
+    def per_row(i):
+        v = jnp.concatenate([info_tx[i], info_rx[i]], axis=0)
+        return jnp.broadcast_to(v[:, None, :], (pair, SAMPLES, 128)).reshape(2 * rows, 128)
+
+    target = per_row(0) + sample
+    live_c = per_row(1)
     for p in range(n):
         gm[p] = jnp.where(target[:, :chunk] == ids_m[p:p + 1, :chunk], 1.0, 0.0).astype(BF16)
 
@@ -257,73 +260,22 @@
             if i == 0:
                 start(second(src, s, 2, 3, piece))
             start(second(src, s, 1, 2, piece))
-            start(forward(src, piece))
-    pick[0] = dot(gm[p2], agm[p2])
-    for i in range(2):
-        for s in range(2):
-            piece = i ^ s
-            start(forward(arrived(s, 0, piece), piece))
-    for p in range(n):
-        go[p] = jnp.where(target[:, :chunk] == ids_o[p:p + 1, :chunk], 1.0, 0.0).astype(BF16)
-    for s in range(2):
-        for dd in (2, 1):
-            src = near(-(1, -1)[s] * dd)
-            pick[0] += dot(gm[src], agm[src])
-
-    def from_core(pos, first_one=False):
-        for piece in range(2):
-            forward(pos, piece).wait_recv()
-        got = dot(go[pos], ago[pos])
-        pick[1] = got if first_one else pick[1] + got
-
-    from_core(p1, True)
-    for dd in (2, -2, 1, -1):
-        from_core(lax.rem(p1 + dd + n, n))
-    for i in range(2):
-        for s in range(2):
-            piece = i ^ s
-            start(forward(arrived(s, 2, piece), piece))
-    for s in range(2):
-        src = near(-(1, -1)[s] * 3)
-        pick[0] += dot(gm[src], agm[src])
-    for s in range(2):
-        start(forward(arrived(s, 3, s), s))
-    src = near(4)
-    pick[0] += dot(gm[src], agm[src])
-    for dd in (3, -3, 4):
-        from_core(lax.rem(p1 + dd + n, n))
-
-    loads[0].wait()
-    blocks = pages // 8
-    scores, peaks = [], []
-    page_l = lax.shift_right_logical(iota((PAGE, 512), 1) & 127, 4)
-    for blk in range(blocks):
-        keys = poolv[blk * 8:(blk + 1) * 8].reshape(8 * PAGE, 2 * HEAD)[:, :HEAD]
-        qb = jnp.concatenate(
-            [
-                pick[h, blk * 128:(blk + 1) * 128, c * HEAD:(c + 1) * HEAD].astype(BF16)
-                for h in range(2) for c in range(2)
-            ],
-            axis=0,
-        )
-        full = dot(keys, qb, 1, 1)
-        s = jnp.zeros((PAGE, 512), F32)
-        for j in range(8):
-            s = jnp.where(page_l == j, full[j * PAGE:(j + 1) * PAGE], s)
-        lv = jnp.concatenate([live_row[:, blk * 128:(blk + 1) * 128]] * 4, axis=1)
-        alive = iota((PAGE, 512), 0).astype(F32) < lv
-        s = jnp.where(alive, s * scale, NEG)
-        scores.append((s, alive))
-        m = jnp.max(s, axis=0, keepdims=True)
-        peaks.append(jnp.concatenate([m[:, i * 128:(i + 1) * 128] for i in range(4)], axis=0))
-    local = jnp.concatenate(peaks, axis=1)
-    peak_tx[...] = jnp.concatenate([local[2:4], local[0:2], local], axis=0)
-    start(remote(peak_tx, peak_rx, cx_send.at[1], cx_recv.at[1], partner))
-
-    remote(ptgt.at[0], ptgt.at[1], cx_send.at[0], cx_recv.at[0], partner).wait_recv()
-    tgt_p = ptgt[1]
-    both_t = jnp.concatenate([target_row[0:4], tgt_p[0:4]], axis=0)
-    swap_t = jnp.concatenate([tgt_p[0:4], target_row[0:4]], axis=0)
+    pick[...] = dot(gm[p2], agm[p2])
+
+    def take(d):
+        src = near(d)
+        pick[...] += dot(gm[src], agm[src])
+
+    for s in range(2):
+        take((-2, 2)[s])
+    target_row = jnp.concatenate(
+        [jnp.transpose(target[i * 128:(i + 1) * 128])[0:8] for i in range(2 * rows // 128)], axis=1
+    )
+    live_row = jnp.concatenate(
+        [jnp.transpose(live_c[i * 128:(i + 1) * 128])[0:1] for i in range(2 * rows // 128)], axis=1
+    )
+    both_t = jnp.concatenate([target_row[0:4, :rows], target_row[0:4, rows:]], axis=0)
+    swap_t = jnp.concatenate([target_row[0:4, rows:], target_row[0:4, :rows]], axis=0)
     lane8 = iota((8, rows), 1)
     lower = iota((8, rows), 0) >= 4
     lead = jnp.where(lower & (swap_t == both_t), 0.0, 1.0)
@@ -331,10 +283,49 @@
         same = pltpu.roll(both_t, d * SAMPLES, 1) == both_t
         cross = pltpu.roll(swap_t, d * SAMPLES, 1) == both_t
         lead = jnp.where((same & (lane8 >= d * SAMPLES)) | (cross & lower), 0.0, lead)
-    remote(peak_tx, peak_rx, cx_send.at[1], cx_recv.at[1], partner).wait_recv()
-    peer = peak_rx[...]
-    both_m = jnp.concatenate([local, peer[0:4]], axis=0)
-    swap_m = jnp.concatenate([peer[0:4], local], axis=0)
+    ids_t = jnp.transpose(jnp.concatenate([ids_m, jnp.zeros((128 - n, 128), F32)], axis=0))
+    for p in range(n):
+        gt[pl.ds(p * chunk, chunk), :] = jnp.where(
+            ids_t[:chunk, p:p + 1] == target_row[0:1], 1.0, 0.0
+        ).astype(BF16)
+    for i in range(2):
+        for s in range(2):
+            arrived(s, 0, i ^ s)
+    for s in range(2):
+        take((-1, 1)[s])
+    for i in range(2):
+        for s in range(2):
+            arrived(s, 2, i ^ s)
+    for s in range(2):
+        take((-3, 3)[s])
+    for s in range(2):
+        arrived(s, 3, s)
+    take(4)
+
+    loads[4].wait()
+    swap.wait_recv()
+    blocks = pair // 8
+    scores, peaks = [], []
+    page_l = lax.shift_right_logical(iota((PAGE, 256), 1) & 127, 4)
+    for blk in range(blocks):
+        keys = poolv[blk * 8:(blk + 1) * 8].reshape(8 * PAGE, 2 * HEAD)[:, :HEAD]
+        sl = slice(blk * 128, (blk + 1) * 128)
+        qb = jnp.concatenate([pick[sl, :HEAD], pick[sl, HEAD:]], axis=0).astype(BF16)
+        full = dot(keys, qb, 1, 1)
+        s = jnp.zeros((PAGE, 256), F32)
+        for j in range(8):
+            s = jnp.where(page_l == j, full[j * PAGE:(j + 1) * PAGE], s)
+        lv = jnp.concatenate([live_row[:, sl]] * 2, axis=1)
+        alive = iota((PAGE, 256), 0).astype(F32) < lv
+        s = jnp.where(alive, s * scale, NEG)
+        scores.append((s, alive))
+        m = jnp.max(s, axis=0, keepdims=True)
+        peaks.append(jnp.concatenate([m[:, :128], m[:, 128:]], axis=0))
+    hb = blocks // 2
+    low, high = jnp.concatenate(peaks[:hb], axis=1), jnp.concatenate(peaks[hb:], axis=1)
+
+    both_m = jnp.concatenate([low, low, high, high], axis=0)
+    swap_m = jnp.concatenate([high, high, low, low], axis=0)
     top = jnp.where(swap_t == both_t, jnp.maximum(both_m, swap_m), both_m)
     for d in range(1, pages):
         same = pltpu.roll(both_t, d * SAMPLES, 1) == both_t
@@ -342,56 +333,35 @@
         top = jnp.where(same, jnp.maximum(top, pltpu.roll(both_m, d * SAMPLES, 1)), top)
         top = jnp.where(cross, jnp.maximum(top, pltpu.roll(swap_m, d * SAMPLES, 1)), top)
 
-    def give(blk):
-        sl = pl.ds(blk * 128, 128)
-        return remote(
-            acco.at[sl], accm.at[pl.ds(rows + blk * 128, 128)], cx_send.at[3 + blk], cx_recv.at[3 + blk],
-            partner,
-        )
-
     dens = []
+    page_r8 = lax.shift_right_logical(iota((256, 8 * PAGE), 0) & 127, 4)
+    own_page = page_r8 == lax.shift_right_logical(iota((256, 8 * PAGE), 1), 6)
     for blk in range(blocks):
         s, alive = scores[blk]
-        tb = top[:, blk * 128:(blk + 1) * 128]
-        tb = jnp.concatenate([tb[i:i + 1] for i in range(4)], axis=1)
+        base = 4 * (blk // hb)
+        tb = top[base:base + 2, (blk % hb) * 128:(blk % hb + 1) * 128]
+        tb = jnp.concatenate([tb[0:1], tb[1:2]], axis=1)
         w = jnp.where(alive, jnp.exp(s - tb), 0.0)
         dsum = jnp.sum(w, axis=0, keepdims=True)
-        dens.append(jnp.concatenate([dsum[:, i * 128:(i + 1) * 128] for i in range(4)], axis=0))
-        wide = jnp.concatenate([jnp.where(page_l == j, w, 0.0) for j in range(8)], axis=0)
+        dens.append(jnp.concatenate([dsum[:, :128], dsum[:, 128:]], axis=0))
+        wt = jnp.transpose(w)
+        wt = jnp.concatenate([wt, wt], axis=1)
+        wide = jnp.where(own_page, jnp.concatenate([wt] * 4, axis=1), 0.0).astype(BF16)
         values = poolv[blk * 8:(blk + 1) * 8].reshape(8 * PAGE, 2 * HEAD)[:, HEAD:]
-        acc = dot(jnp.transpose(wide).astype(BF16), values)
-        for c in range(2):
-            acco[blk * 128:(blk + 1) * 128, c * HEAD:(c + 1) * HEAD] = (
-                acc[(2 + c) * 128:(3 + c) * 128].astype(BF16)
-            )
-        start(give(blk))
-        for c in range(2):
-            accm[blk * 128:(blk + 1) * 128, c * HEAD:(c + 1) * HEAD] = (
-                acc[c * 128:(c + 1) * 128].astype(BF16)
-            )
-    den = jnp.concatenate(dens, axis=1)
-    den_tx[...] = jnp.concatenate([den[2:4], den[2:4], den], axis=0)
-    start(remote(den_tx, den_rx, cx_send.at[2], cx_recv.at[2], partner))
-    for p in range(n):
-        if p == 0:
-            ids_t = jnp.transpose(jnp.concatenate([ids_m, jnp.zeros((128 - n, 128), F32)], axis=0))
-            all_t = jnp.concatenate([target_row[0:1], tgt_p[0:1]], axis=1)
-        gt[pl.ds(p * chunk, chunk), :] = jnp.where(ids_t[:chunk, p:p + 1] == all_t, 1.0, 0.0).astype(BF16)
-    remote(den_tx, den_rx, cx_send.at[2], cx_recv.at[2], partner).wait_recv()
-    den_p = den_rx[...]
+        acc = dot(wide, values).astype(BF16)
+        accm[blk * 128:(blk + 1) * 128, :HEAD] = acc[:128]
+        accm[blk * 128:(blk + 1) * 128, HEAD:] = acc[128:]
     st = jnp.concatenate(
         [
             jnp.concatenate([jnp.where(lead[0:2] > 0.5, top[0:2], 0.0),
                              jnp.where(lead[4:6] > 0.5, top[4:6], 0.0)], axis=1),
-            jnp.concatenate([den[0:2], den_p[0:2]], axis=1),
+            jnp.concatenate(dens, axis=1),
             jnp.concatenate([lead[0:1], lead[4:5]], axis=1),
             jnp.zeros((3, 2 * rows), F32),
         ],
         axis=0,
     )
     stats[...] = jnp.concatenate(split3(st), axis=0).astype(BF16)
-    for blk in range(blocks):
-        give(blk).wait_recv()
 
     sub8 = iota((8, 128), 0)
 
@@ -476,7 +446,9 @@
             start(copy)
     home_acc, home_ml = sums(0)
 
-    loads[1].wait()
+    loads[5].wait()
+    loads[6].wait()
+    loads[7].wait()
     qown = jnp.concatenate([q_ref[0], q_ref[1]], axis=0)
     tails = tailv[...].reshape(reqs * 128, 2 * HEAD)
     row32 = iota((32, 128), 0) & 7
@@ -538,7 +510,7 @@
             start(home(pos, kk))
     start(home(p1, other))
     r2[k, p1] = t2[p1 * 2 + k]
-    loads[2].wait()
+    loads[8].wait()
     for d in range(1, n):
         for h in range(2):
             src = lax.rem((y, z)[h] + d, n)
@@ -566,29 +538,50 @@
         [jnp.concatenate([a[0:8], a[8:16]], axis=1) for a in heads], axis=0
     ).astype(BF16)
 
-    ar[x] = dot(att, wv[...]).astype(BF16)
-
-    def share(d):
-        return remote(
-            ar.at[x], ar.at[x], ar_send.at[d], ar_recv.at[x], (lax.rem(x + d, nx), b)
-        )
-
-    for d in range(1, nx):
-        start(share(d))
-    raw_h = hid_ref[...].astype(F32)
-    for d in range(1, nx):
-        src = lax.rem(x + nx - d, nx)
-        remote(ar.at[src], ar.at[src], ar_send.at[d], ar_recv.at[src], partner).wait_recv()
-    total_h = ar[0].astype(F32)
-    for i in range(1, nx):
-        total_h += ar[i].astype(F32)
-    hid = [(raw_h[:, i, :] + total_h[8 * i:8 * i + reqs]).astype(BF16).astype(F32) for i in range(2)]
+    hw = wv.shape[1] // 2
+    even = x + 1 - 2 * lax.rem(x, 2)
+    odd = nx - 1 - x
+    if nx == 1:
+        for i in range(2):
+            out_ref[0, i] = dot(att, wv[:, i * hw:(i + 1) * hw]).astype(BF16)
+            out_ref[1, i] = jnp.zeros((16, hw), BF16)
+    else:
+        def trade(i, turn):
+            src = ar.at[i] if turn == 0 else out_ref.at[0, i]
+            dst = ar_rx.at[i] if turn == 0 else out_ref.at[1, i]
+            to = even if (i + turn) % 2 == 0 else odd
+            return remote(src, dst, ar_send.at[turn, i], ar_recv.at[turn, i], (to, b))
+
+        for i in range(2):
+            ar[i] = dot(att, wv[:, i * hw:(i + 1) * hw]).astype(BF16)
+            start(trade(i, 0))
+        for i in range(2):
+            trade(i, 0).wait_recv()
+            out_ref[0, i] = (ar[i].astype(F32) + ar_rx[i].astype(F32)).astype(BF16)
+            if nx > 2:
+                start(trade(i, 1))
+            else:
+                out_ref[1, i] = jnp.zeros((16, hw), BF16)
+        for i in range(2):
+            if nx > 2:
+                trade(i, 1).wait_recv()
+    for copy in pending:
+        copy.wait_send()
+
+
+def finish(sum_ref, hid_ref, gain_ref, score_ref, out_ref, sc_ref):
+    reqs = hid_ref.shape[0]
+    raw = hid_ref[...].astype(F32)
+    total = jnp.concatenate(
+        [sum_ref[0, i].astype(F32) + sum_ref[1, i].astype(F32) for i in range(2)], axis=1
+    )
+    hid = [(raw[:, i, :] + total[8 * i:8 * i + reqs]).astype(BF16).astype(F32) for i in range(2)]
     out_ref[...] = jnp.stack(hid, axis=1).astype(BF16)
     last = hid[1]
     normed = last * lax.rsqrt(jnp.mean(last * last, axis=1, keepdims=True) + 1e-06) * gain_ref[...]
-    sc_ref[...] = jnp.broadcast_to(jnp.sum(normed * score_ref[...], axis=1, keepdims=True), (reqs, 128))
-    for copy in pending:
-        copy.wait_send()
+    score = jnp.sum(normed * score_ref[...], axis=1, keepdims=True)
+    tile = jnp.concatenate([jnp.broadcast_to(score, (reqs, 128)), jnp.zeros((128 - reqs, 128), F32)], axis=0)
+    sc_ref[...] = jnp.transpose(tile)[0, :reqs]
 
 
 def p1_of(y, z, h):
@@ -603,37 +596,33 @@
     rows = pages * SAMPLES
     total = n * chunk
     vm = pl.BlockSpec(memory_space=pltpu.VMEM)
-    sm = pl.BlockSpec(memory_space=pltpu.SMEM)
     hbm = pl.BlockSpec(memory_space=pl.ANY)
     dma = pltpu.SemaphoreType.DMA
-    out, sc = pl.pallas_call(
+    sums = pl.pallas_call(
         functools.partial(kernel, n, nx, reqs, pages),
-        out_shape=(
-            jax.ShapeDtypeStruct((reqs, 2, width), BF16),
-            jax.ShapeDtypeStruct((reqs, 128), F32),
-        ),
-        in_specs=[sm, sm, sm, vm, vm, vm, vm, vm, vm, hbm, hbm, hbm],
-        out_specs=(vm, vm),
+        out_shape=jax.ShapeDtypeStruct((2, 2, 16, width // 2), BF16),
+        in_specs=[hbm] * 9,
+        out_specs=vm,
         scratch_shapes=[
+            pltpu.SMEM(slot_page.shape, jnp.int32),
+            pltpu.SMEM(prompt_len.shape, jnp.int32),
+            pltpu.SMEM(tail_len.shape, jnp.int32),
+            pltpu.VMEM(request_ids.shape, jnp.int32),
+            pltpu.VMEM(queries.shape, BF16),
+            pltpu.VMEM(new_kv.shape[1:], BF16),
             pltpu.VMEM((2, 16, HEAD), BF16),
-            pltpu.VMEM((pages, PAGE, 2 * HEAD), BF16),
+            pltpu.VMEM((2 * pages, PAGE, 2 * HEAD), BF16),
             pltpu.VMEM((reqs, 128, 2 * HEAD), BF16),
             pltpu.VMEM((2 * HEAD, width), BF16),
             pltpu.VMEM((2 * n, 16, HEAD), BF16),
             pltpu.VMEM((n, chunk, 512), BF16),
-            pltpu.VMEM((n, chunk, 512), BF16),
-            pltpu.VMEM((n, rows, chunk), BF16),
-            pltpu.VMEM((n, rows, chunk), BF16),
+            pltpu.VMEM((n, 2 * rows, chunk), BF16),
             pltpu.VMEM((total, 2 * rows), BF16),
-            pltpu.VMEM((2, rows, 512), F32),
+            pltpu.VMEM((2 * rows, 512), F32),
             pltpu.VMEM((2 * rows, 512), BF16),
-            pltpu.VMEM((rows, 512), BF16),
             pltpu.VMEM((24, 2 * rows), BF16),
-            pltpu.VMEM((2, 8, rows), F32),
-            pltpu.VMEM((8, rows), F32),
-            pltpu.VMEM((8, rows), F32),
-            pltpu.VMEM((8, rows), F32),
-            pltpu.VMEM((8, rows), F32),
+            pltpu.VMEM((2, pages, 128), F32),
+            pltpu.VMEM((2, pages, 128), F32),
             pltpu.VMEM((7, chunk, 512), BF16),
             pltpu.VMEM((7, 8, 128), F32),
             pltpu.VMEM((2, chunk, 512), BF16),
@@ -644,19 +633,25 @@
             pltpu.VMEM((2, n, 16, HEAD + 128), BF16),
             pltpu.VMEM((32, HEAD), F32),
             pltpu.VMEM((32, 128), F32),
-            pltpu.VMEM((nx, 16, width), BF16),
-            dma((3,)), dma((2 * n,)), dma((2 * n,)),
-            dma((2, 4, 2)), dma((2, 4, 2)), dma((n, 2)), dma((n, 2)),
-            dma((3 + pages // 8,)), dma((3 + pages // 8,)),
+            pltpu.VMEM((2, 16, width // 2), BF16),
+            pltpu.VMEM((2, 16, width // 2), BF16),
+            dma((9,)), dma((2 * n,)), dma((2 * n,)),
+            dma((2, 4, 2)), dma((2, 4, 2)),
+            dma((2,)), dma((2,)),
             dma((2, 4)), dma((2, 4)), dma((2, 4)), dma((2, 4)),
-            dma((2 * n,)), dma((2, n)), dma((nx,)), dma((nx,)),
+            dma((2 * n,)), dma((2, n)), dma((2, 2)), dma((2, 2)),
         ],
         compiler_params=pltpu.CompilerParams(collective_id=0, has_side_effects=True),
     )(
-        slot_page, prompt_len, tail_len, request_ids.reshape(1, -1), queries, new_kv[0], hidden,
-        norm_gain.reshape(1, -1), score_weight.reshape(1, -1), prefix_pool[0], tail_cache[0], out_weight,
-    )
-    return out, sc[:, 0]
+        slot_page, prompt_len, tail_len, request_ids, queries, new_kv[0],
+        prefix_pool[0], tail_cache[0], out_weight,
+    )
+    return pl.pallas_call(
+        finish,
+        out_shape=(jax.ShapeDtypeStruct(hidden.shape, BF16), jax.ShapeDtypeStruct((reqs,), F32)),
+        in_specs=[vm] * 4,
+        out_specs=(vm, vm),
+    )(sums, hidden, norm_gain.reshape(1, -1), score_weight.reshape(1, -1))
 
 
 def solution(mesh):

time: 65.8 us -> 59.3 us (0.901)
  local copies, waits for them, and re-layouts: 4.03 us -> 0 us
  Pallas kernels: 60.9 us -> 57.8 us
    pallas_call x1 -> x2, Pallas kernels: 60.9 us -> 57.8 us  [the longest x1 55.9 us: body(): pl.pallas_call(functools.partial(kernel, n, nx, reqs, pages), out_shape=j...]
    unnamed x1 -> x0, local copies, waits for them, and re-layouts: 1.45 us -> none
    slice x1 -> x0, local copies, waits for them, and re-layouts: 1.31 us -> none  [body(): return (out, sc[:, 0])]
    reshape x1 -> x0, local copies, waits for them, and re-layouts: 1.27 us -> none  [body(): request_ids.reshape(1, -1)]
where the time goes in v3:
time: 59.3 us; the launch traced here: 58.5 us
  Pallas kernels  57.8 us (97%)
  between operations  0.64 us (1%)
    pallas_call x1, Pallas kernels, body(): pl.pallas_call(functools.partial(kernel, n, nx, reqs, pages), out_shape=j...  55.9 us
    pallas_call x1, Pallas kernels, body(): pl.pallas_call(finish, out_shape=(jax.ShapeDtypeStruct(hidden.shape, BF16...  1.9 us

profile of v3, /device:TPU:1, one launch (start us, length us, event | category | flops | bytes accessed | tf_op | source)
XLA Modules:
  0.0 58.5 jit_solution(11546047100693083225)
XLA Ops:
  0.6 55.9 %shard_map.131.sum_ref = bf16[2,2,16,1024]{3,2,1,0:T(8,128)(2,1)} custom-call(s32[24]{0:T(128)} %slot_hbm.1, s32[48]{0:T(128)} %plen_hbm.1, s32[6]{0:T(128)} %tlen_hbm.1, s32[768]{0:T(1024)} %ids_hbm.1, bf16[6,2,512]{2,1,0:T(2,128)(2,1)} %q_hbm.1, bf16[6,2,512]{2,1,0:T(2,128)(2,1)} %bitcast.7, bf16[24,64,512]{2,1,0:T(8,128)(2,1)} %bitcast.5, ...), custom_call_target="tpu_custom_call" | custom-call | tf_op jit(solution)/shard_map/pallas_call | solution.py:601
  56.6 1.9 %shard_map.132 = (bf16[6,2,2048]{2,1,0:T(2,128)(2,1)}, f32[6]{0:T(128)}) custom-call(bf16[2,2,16,1024]{3,2,1,0:T(8,128)(2,1)} %shard_map.131.sum_ref, bf16[6,2,2048]{2,1,0:T(2,128)(2,1)} %hid_ref.1, f32[1,2048]{1,0:T(1,128)} %bitcast.8, f32[1,2048]{1,0:T(1,128)} %bitcast.9), custom_call_target="tpu_custom_call" | custom-call | tf_op jit(solution)/shard_map/pallas_call | solution.py:649

commit v4 on v3

--- a/solution.py
+++ b/solution.py
@@ -600,7 +600,7 @@
     dma = pltpu.SemaphoreType.DMA
     sums = pl.pallas_call(
         functools.partial(kernel, n, nx, reqs, pages),
-        out_shape=jax.ShapeDtypeStruct((2, 2, 16, width // 2), BF16),
+        out_shape=pltpu.VMEM((2, 2, 16, width // 2), BF16),
         in_specs=[hbm] * 9,
         out_specs=vm,
         scratch_shapes=[
@@ -651,7 +651,7 @@
         out_shape=(jax.ShapeDtypeStruct(hidden.shape, BF16), jax.ShapeDtypeStruct((reqs,), F32)),
         in_specs=[vm] * 4,
         out_specs=(vm, vm),
-    )(sums, hidden, norm_gain.reshape(1, -1), score_weight.reshape(1, -1))
+    )(pltpu.with_memory_space_constraint(sums, pltpu.VMEM), hidden, norm_gain.reshape(1, -1), score_weight.reshape(1, -1))
 
 
 def solution(mesh):

time: 59.3 us -> 58.6 us (0.988)
  Pallas kernels: 57.8 us -> 57.1 us
    pallas_call x1, Pallas kernels: 55.9 us -> 55.3 us  [body(): pl.pallas_call(functools.partial(kernel, n, nx, reqs, pages), out_shape=p...]
where the time goes in v4:
time: 58.6 us; the launch traced here: 57.7 us
  Pallas kernels  57.1 us (97%)
  between operations  0.64 us (1%)
    pallas_call x1, Pallas kernels, body(): pl.pallas_call(functools.partial(kernel, n, nx, reqs, pages), out_shape=p...  55.3 us
    pallas_call x1, Pallas kernels, body(): pl.pallas_call(finish, out_shape=(jax.ShapeDtypeStruct(hidden.shape, BF16...  1.77 us

profile of v4, /device:TPU:1, one launch (start us, length us, event | category | flops | bytes accessed | tf_op | source)
XLA Modules:
  0.0 57.7 jit_solution(9336230645306175343)
XLA Ops:
  0.6 55.3 %shard_map.131.sum_ref = bf16[2,2,16,1024]{3,2,1,0:T(8,128)(2,1)S(1)} custom-call(s32[24]{0:T(128)} %slot_hbm.1, s32[48]{0:T(128)} %plen_hbm.1, s32[6]{0:T(128)} %tlen_hbm.1, s32[768]{0:T(1024)} %ids_hbm.1, bf16[6,2,512]{2,1,0:T(2,128)(2,1)} %q_hbm.1, bf16[6,2,512]{2,1,0:T(2,128)(2,1)} %bitcast.7, bf16[24,64,512]{2,1,0:T(8,128)(2,1)} %bitcast.5, ...), custom_call_target="tpu_custom_call" | custom-call | tf_op jit(solution)/shard_map/pallas_call | solution.py:601
  55.9 1.8 %shard_map.132 = (bf16[6,2,2048]{2,1,0:T(2,128)(2,1)}, f32[6]{0:T(128)}) custom-call(bf16[2,2,16,1024]{3,2,1,0:T(8,128)(2,1)S(1)} %shard_map.131.sum_ref, bf16[6,2,2048]{2,1,0:T(2,128)(2,1)} %hid_ref.1, f32[1,2048]{1,0:T(1,128)} %bitcast.8, f32[1,2048]{1,0:T(1,128)} %bitcast.9), custom_call_target="tpu_custom_call" | custom-call | tf_op jit(solution)/shard_map/pallas_call | solution.py:649

commit v5 on v4

--- a/solution.py
+++ b/solution.py
@@ -37,7 +37,8 @@
 def kernel(
     n, nx, reqs, pages,
     slot_hbm, plen_hbm, tlen_hbm, ids_hbm, q_hbm, nk_hbm, pool_hbm, tail_hbm, w_hbm,
-    out_ref,
+    hid_hbm, gain_hbm, score_hbm,
+    out_ref, hid_out, gain_out, score_out,
     slot_ref, plen_ref, tlen_ref, ids_ref, q_in, nk_ref,
     q_ref, poolv, tailv, wv, s1, agm, gm, gt, pick, accm, stats, info_tx, info_rx,
     tx_acc, tx_ml, a3_acc, a4_acc, b_acc, rx_ml, t2, r2, own_acc, own_st, ar, ar_rx,
@@ -111,6 +112,7 @@
             (q_hbm, q_in), (plen_hbm, plen_ref), (slot_hbm, slot_ref), (ids_hbm, ids_ref),
             (pool_hbm, poolv.at[pl.ds(0, pages)]), (tlen_hbm, tlen_ref), (nk_hbm, nk_ref),
             (tail_hbm, tailv), (w_hbm, wv),
+            (hid_hbm, hid_out), (gain_hbm, gain_out), (score_hbm, score_out),
         ])
     ]
     for load in loads:
@@ -565,6 +567,8 @@
         for i in range(2):
             if nx > 2:
                 trade(i, 1).wait_recv()
+    for load in loads[9:]:
+        load.wait()
     for copy in pending:
         copy.wait_send()
 
@@ -600,9 +604,14 @@
     dma = pltpu.SemaphoreType.DMA
     sums = pl.pallas_call(
         functools.partial(kernel, n, nx, reqs, pages),
-        out_shape=pltpu.VMEM((2, 2, 16, width // 2), BF16),
-        in_specs=[hbm] * 9,
-        out_specs=vm,
+        out_shape=(
+            pltpu.VMEM((2, 2, 16, width // 2), BF16),
+            pltpu.VMEM(hidden.shape, BF16),
+            pltpu.VMEM((1, width), F32),
+            pltpu.VMEM((1, width), F32),
+        ),
+        in_specs=[hbm] * 12,
+        out_specs=(vm,) * 4,
         scratch_shapes=[
             pltpu.SMEM(slot_page.shape, jnp.int32),
             pltpu.SMEM(prompt_len.shape, jnp.int32),
@@ -635,7 +644,7 @@
             pltpu.VMEM((32, 128), F32),
             pltpu.VMEM((2, 16, width // 2), BF16),
             pltpu.VMEM((2, 16, width // 2), BF16),
-            dma((9,)), dma((2 * n,)), dma((2 * n,)),
+            dma((12,)), dma((2 * n,)), dma((2 * n,)),
             dma((2, 4, 2)), dma((2, 4, 2)),
             dma((2,)), dma((2,)),
             dma((2, 4)), dma((2, 4)), dma((2, 4)), dma((2, 4)),
@@ -644,14 +653,15 @@
         compiler_params=pltpu.CompilerParams(collective_id=0, has_side_effects=True),
     )(
         slot_page, prompt_len, tail_len, request_ids, queries, new_kv[0],
-        prefix_pool[0], tail_cache[0], out_weight,
+        prefix_pool[0], tail_cache[0], out_weight, hidden, norm_gain.reshape(1, -1),
+        score_weight.reshape(1, -1),
     )
     return pl.pallas_call(
         finish,
         out_shape=(jax.ShapeDtypeStruct(hidden.shape, BF16), jax.ShapeDtypeStruct((reqs,), F32)),
         in_specs=[vm] * 4,
         out_specs=(vm, vm),
-    )(pltpu.with_memory_space_constraint(sums, pltpu.VMEM), hidden, norm_gain.reshape(1, -1), score_weight.reshape(1, -1))
+    )(*(pltpu.with_memory_space_constraint(a, pltpu.VMEM) for a in sums))
 
 
 def solution(mesh):

time: 58.6 us -> 57.8 us (0.986)
  Pallas kernels: 57.1 us -> 56.3 us
    pallas_call x1, Pallas kernels: 1.77 us -> 0.96 us  [body(): pl.pallas_call(finish, out_shape=(jax.ShapeDtypeStruct(hidden.shape, BF16...]
where the time goes in v5:
time: 57.8 us; the launch traced here: 56.9 us
  Pallas kernels  56.3 us (97%)
  between operations  0.64 us (1%)
    pallas_call x1, Pallas kernels, body(): pl.pallas_call(functools.partial(kernel, n, nx, reqs, pages), out_shape=(...  55.3 us

profile of v5, /device:TPU:1, one launch (start us, length us, event | category | flops | bytes accessed | tf_op | source)
XLA Modules:
  0.0 56.9 jit_solution(18182425014576811319)
XLA Ops:
  0.6 55.3 %shard_map.131 = (bf16[2,2,16,1024]{3,2,1,0:T(8,128)(2,1)S(1)}, bf16[6,2,2048]{2,1,0:T(2,128)(2,1)S(1)}, f32[1,2048]{1,0:T(1,128)S(1)}, f32[1,2048]{1,0:T(1,128)S(1)}) custom-call(s32[24]{0:T(128)} %slot_hbm.1, s32[48]{0:T(128)} %plen_hbm.1, s32[6]{0:T(128)} %tlen_hbm.1, s32[768]{0:T(1024)} %ids_hbm.1, bf16[6,2,512]{2,1,0:T(2,128)(2,1)} %q_hbm.1, ...), custom_call_target="tpu_custom_call" | custom-call | tf_op jit(solution)/shard_map/pallas_call | solution.py:605
  56.0 1.0 %shard_map.132 = (bf16[6,2,2048]{2,1,0:T(2,128)(2,1)}, f32[6]{0:T(128)}) custom-call(bf16[2,2,16,1024]{3,2,1,0:T(8,128)(2,1)S(1)} %get-tuple-element.6.sum_ref, bf16[6,2,2048]{2,1,0:T(2,128)(2,1)S(1)} %get-tuple-element.7.hid_ref, f32[1,2048]{1,0:T(1,128)S(1)} %get-tuple-element.8.gain_ref, f32[1,2048]{1,0:T(1,128)S(1)} %get-tuple-element.9.score_ref), custom_call_target="tpu_custom_call" | custom-call | tf_op jit(solution)/shard_map/pallas_call | solution.py:659

commit v6 on v5

--- a/solution.py
+++ b/solution.py
@@ -399,10 +399,6 @@
         store(s, (3, -3)[s])
         for copy in ring(s, 0, (tx_acc.at[s], tx_ml.at[s]), a3_acc.at[s], 1):
             start(copy)
-    for s in range(2):
-        store(3 + s, (1, -1)[s])
-        for copy in ring(s, 2, (tx_acc.at[3 + s], tx_ml.at[3 + s]), b_acc.at[s, 0], 1):
-            start(copy)
 
     def weigh(mls):
         out = []
@@ -445,6 +441,10 @@
             [st[0][1], st[1][1], st[0][2], st[1][2], jnp.zeros((4, 128), F32)], axis=0
         )
         for copy in ring(s, 3, (tx_acc.at[5 + s], tx_ml.at[5 + s]), b_acc.at[s, 1], 2):
+            start(copy)
+    for s in range(2):
+        store(3 + s, (1, -1)[s])
+        for copy in ring(s, 2, (tx_acc.at[3 + s], tx_ml.at[3 + s]), b_acc.at[s, 0], 1):
             start(copy)
     home_acc, home_ml = sums(0)
 

time: 57.8 us -> 60.5 us (1.047)
  Pallas kernels: 56.3 us -> 59.1 us
    pallas_call x1, Pallas kernels: 55.3 us -> 58.2 us  [body(): pl.pallas_call(functools.partial(kernel, n, nx, reqs, pages), out_shape=(...]
where the time goes in v6:
time: 60.5 us; the launch traced here: 59.8 us
  Pallas kernels  59.1 us (98%)
  between operations  0.64 us (1%)
    pallas_call x1, Pallas kernels, body(): pl.pallas_call(functools.partial(kernel, n, nx, reqs, pages), out_shape=(...  58.2 us

profile of v6, /device:TPU:1, one launch (start us, length us, event | category | flops | bytes accessed | tf_op | source)
XLA Modules:
  0.0 59.8 jit_solution(7462226231012300654)
XLA Ops:
  0.6 58.2 %shard_map.131 = (bf16[2,2,16,1024]{3,2,1,0:T(8,128)(2,1)S(1)}, bf16[6,2,2048]{2,1,0:T(2,128)(2,1)S(1)}, f32[1,2048]{1,0:T(1,128)S(1)}, f32[1,2048]{1,0:T(1,128)S(1)}) custom-call(s32[24]{0:T(128)} %slot_hbm.1, s32[48]{0:T(128)} %plen_hbm.1, s32[6]{0:T(128)} %tlen_hbm.1, s32[768]{0:T(1024)} %ids_hbm.1, bf16[6,2,512]{2,1,0:T(2,128)(2,1)} %q_hbm.1, ...), custom_call_target="tpu_custom_call" | custom-call | tf_op jit(solution)/shard_map/pallas_call | solution.py:605
  58.8 1.0 %shard_map.132 = (bf16[6,2,2048]{2,1,0:T(2,128)(2,1)}, f32[6]{0:T(128)}) custom-call(bf16[2,2,16,1024]{3,2,1,0:T(8,128)(2,1)S(1)} %get-tuple-element.6.sum_ref, bf16[6,2,2048]{2,1,0:T(2,128)(2,1)S(1)} %get-tuple-element.7.hid_ref, f32[1,2048]{1,0:T(1,128)S(1)} %get-tuple-element.8.gain_ref, f32[1,2048]{1,0:T(1,128)S(1)} %get-tuple-element.9.score_ref), custom_call_target="tpu_custom_call" | custom-call | tf_op jit(solution)/shard_map/pallas_call | solution.py:659

commit v7 on v5

--- a/solution.py
+++ b/solution.py
@@ -419,8 +419,9 @@
         )
 
     lane128 = iota((8, 128), 1)
-    for s in range(2):
-        acc, ml = sums((2, -2)[s])
+    own2 = [sums(2), sums(-2)]
+    for s in range(2):
+        acc, ml = own2[s]
         landed(s, 0, a3_acc.at[s])
         landed(s, 1, a4_acc.at[s])
         inside = (lane128 < half) if s == 0 else (lane128 >= half)

time: 57.8 us -> 57.9 us (level)
  no operation moved by 1% of the time
where the time goes in v7:
time: 57.9 us; the launch traced here: 57.5 us
  Pallas kernels  56.8 us (98%)
  between operations  0.64 us (1%)
    pallas_call x1, Pallas kernels, body(): pl.pallas_call(functools.partial(kernel, n, nx, reqs, pages), out_shape=(...  55.9 us

profile of v7, /device:TPU:1, one launch (start us, length us, event | category | flops | bytes accessed | tf_op | source)
XLA Modules:
  0.0 57.5 jit_solution(14108979891044674708)
XLA Ops:
  0.6 55.9 %shard_map.131 = (bf16[2,2,16,1024]{3,2,1,0:T(8,128)(2,1)S(1)}, bf16[6,2,2048]{2,1,0:T(2,128)(2,1)S(1)}, f32[1,2048]{1,0:T(1,128)S(1)}, f32[1,2048]{1,0:T(1,128)S(1)}) custom-call(s32[24]{0:T(128)} %slot_hbm.1, s32[48]{0:T(128)} %plen_hbm.1, s32[6]{0:T(128)} %tlen_hbm.1, s32[768]{0:T(1024)} %ids_hbm.1, bf16[6,2,512]{2,1,0:T(2,128)(2,1)} %q_hbm.1, ...), custom_call_target="tpu_custom_call" | custom-call | tf_op jit(solution)/shard_map/pallas_call | solution.py:606
  56.5 1.0 %shard_map.132 = (bf16[6,2,2048]{2,1,0:T(2,128)(2,1)}, f32[6]{0:T(128)}) custom-call(bf16[2,2,16,1024]{3,2,1,0:T(8,128)(2,1)S(1)} %get-tuple-element.6.sum_ref, bf16[6,2,2048]{2,1,0:T(2,128)(2,1)S(1)} %get-tuple-element.7.hid_ref, f32[1,2048]{1,0:T(1,128)S(1)} %get-tuple-element.8.gain_ref, f32[1,2048]{1,0:T(1,128)S(1)} %get-tuple-element.9.score_ref), custom_call_target="tpu_custom_call" | custom-call | tf_op jit(solution)/shard_map/pallas_call | solution.py:660
